TPU v7x, 32 devices: a whole 2x2x4 slice. The times are simulated.
32 devices in a mesh: dp: 8 (over z, x), tensor: 4 (over y, core).
Axes of the slice: x: 2, y: 2, z: 4, core: 2. Of those that a mesh axis runs over, the one named last changes fastest.
Arguments:
- layer_in: bfloat16 [32768, 768], P(('dp', 'tensor')), may hold values from -6 to 6
- query_weight: bfloat16 [768, 768], P('dp', 'tensor'), may hold values from -0.3125 to 0.3125
- key_weight: bfloat16 [768, 768], P('dp', 'tensor'), may hold values from -0.3125 to 0.3125
- value_weight: bfloat16 [768, 768], P('dp', 'tensor'), may hold values from -0.21875 to 0.21875
- output_weight: bfloat16 [768, 768], P('tensor', 'dp'), may hold values from -0.875 to 0.875
- inner_weight: bfloat16 [768, 3072], P('dp', 'tensor'), may hold values from -0.21875 to 0.21875
- outer_weight: bfloat16 [3072, 768], P('tensor', 'dp'), may hold values from -0.15625 to 0.15625
- query_bias: float32 [768], P(('dp', 'tensor')), may hold values from -3 to 3
- value_bias: float32 [768], P(('dp', 'tensor')), may hold values from -3 to 3
- output_bias: float32 [768], P(('dp', 'tensor')), may hold values from -3 to 3
- inner_bias: float32 [3072], P(('dp', 'tensor')), may hold values from -3 to 3
- outer_bias: float32 [768], P(('dp', 'tensor')), may hold values from -3 to 3
- first_gain: float32 [768], P(('dp', 'tensor')), may hold values from 0.5 to 1.5
- first_shift: float32 [768], P(('dp', 'tensor')), may hold values from -2 to 2
- second_gain: float32 [768], P(('dp', 'tensor')), may hold values from 0.5 to 1.5
- second_shift: float32 [768], P(('dp', 'tensor')), may hold values from -2 to 2
- segment_ids: int32 [32768], P('dp'), may hold values from 0 to 7, as said below
- pad_mask: int32 [32768], P('dp'), may hold values from 0 to 1, as said below
- random_blocks: int32 [16, 32, 3], P('dp'), may hold values from 0 to 31
- global_blocks: int32 [16, 8, 2], P('dp'), may hold values from 0 to 31, as said below
- output_grad: bfloat16 [32768, 768], P(('dp', 'tensor')), may hold values from -6 to 6
Outputs:
- layer_out: bfloat16 [32768, 768], P(('dp', 'tensor'))
- input_grad: float32 [32768, 768], P(('dp', 'tensor'))
- query_weight_grad: float32 [768, 768], P('dp', 'tensor')
- key_weight_grad: float32 [768, 768], P('dp', 'tensor')
- value_weight_grad: float32 [768, 768], P('dp', 'tensor')
- output_weight_grad: float32 [768, 768], P('tensor', 'dp')
- inner_weight_grad: float32 [768, 3072], P('dp', 'tensor')
- outer_weight_grad: float32 [3072, 768], P('tensor', 'dp')
- query_bias_grad: float32 [768], P(('dp', 'tensor'))
- value_bias_grad: float32 [768], P(('dp', 'tensor'))
- output_bias_grad: float32 [768], P(('dp', 'tensor'))
- inner_bias_grad: float32 [3072], P(('dp', 'tensor'))
- outer_bias_grad: float32 [768], P(('dp', 'tensor'))
- first_gain_grad: float32 [768], P(('dp', 'tensor'))
- first_shift_grad: float32 [768], P(('dp', 'tensor'))
- second_gain_grad: float32 [768], P(('dp', 'tensor'))
- second_shift_grad: float32 [768], P(('dp', 'tensor'))
Inputs may be any that keep to these rules, and one draw needn't show every extreme that they name: `segment_ids`: within each sequence of 2048 tokens the numbers start at 0, never fall and rise by one at each new document; every sequence holds 8 documents; every document but the last of a sequence has 192 tokens or more; padding tokens carry the number of the sequence's last document. `pad_mask`: the padding of a sequence is its last 0 to 127 tokens. `global_blocks`: row s of a sequence holds two block indices for document number s: the first is the block of the document's first token, the second lies one or two blocks after it, or is the last block; the two may be equal.
All inputs are finite; a program needn't handle non-finite values.
Results may differ from a plain program's by a relative error of at most 0.02.
Values may be sent and summed in bfloat16 or wider, within the bound.
A program may use at most 320 MiB of HBM per device.

v0:
```python
from functools import partial

import jax
import jax.numpy as jnp
from jax import lax
from jax.experimental import pallas as pl
from jax.experimental.pallas import tpu as pltpu
from jax.sharding import PartitionSpec as P

HD = 64
PAIR = 2 * HD
QT = 256
KT = 128
ROWS = 256
EPSILON = 1e-06
NEGATIVE = -1e30
MESH = pl.DeviceIdType.MESH
VMEM_LIMIT = 56 * 2**20
BF = jnp.bfloat16
F32 = jnp.float32


def params_of(collective_id=None):
    if collective_id is None:
        return pltpu.CompilerParams(vmem_limit_bytes=VMEM_LIMIT)
    return pltpu.CompilerParams(
        vmem_limit_bytes=VMEM_LIMIT, collective_id=collective_id, has_side_effects=True
    )


def nt(left, right, **more):
    return lax.dot_general(
        left, right, (((1,), (1,)), ((), ())), preferred_element_type=F32, **more
    )


def nn(left, right):
    return lax.dot_general(left, right, (((1,), (0,)), ((), ())), preferred_element_type=F32)


def tn(left, right):
    return lax.dot_general(left, right, (((0,), (0,)), ((), ())), preferred_element_type=F32)


def sibling_of():
    rank = lax.axis_index("tensor")
    half = lax.rem(rank, 2)
    return half, {"tensor": rank + 1 - 2 * half}


def meet(others):
    barrier = pltpu.get_barrier_semaphore()
    for other in others:
        pl.semaphore_signal(barrier, inc=1, device_id=other, device_id_type=MESH)
    pl.semaphore_wait(barrier, len(others))


def swap_keys_kernel(qkv_ref, other_ref, send_sem, recv_sem):
    half, sibling = sibling_of()
    meet([sibling])
    third = qkv_ref.shape[1] // 6
    moves = [
        pltpu.make_async_remote_copy(
            qkv_ref.at[:, (3 * y + 1) * third : (3 * y + 3) * third],
            other_ref.at[:, 2 * y * third : 2 * (y + 1) * third],
            send_sem.at[y], recv_sem.at[y], device_id=sibling, device_id_type=MESH,
        )
        for y in range(2)
    ]
    for move in moves:
        move.start()
    for move in moves:
        move.wait()


def swap_keys(qkv):
    rows, width = qkv.shape
    return pl.pallas_call(
        swap_keys_kernel,
        name="swap_keys",
        out_shape=jax.ShapeDtypeStruct((rows, width * 2 // 3), qkv.dtype),
        in_specs=[pl.BlockSpec(memory_space=pl.ANY)],
        out_specs=pl.BlockSpec(memory_space=pl.ANY),
        scratch_shapes=[pltpu.SemaphoreType.DMA((2,))] * 2,
        compiler_params=params_of(1),
    )(qkv)


def swap_pair_kernel(both_ref, other_ref, send_sem, recv_sem):
    half, sibling = sibling_of()
    meet([sibling])
    away = pltpu.make_async_remote_copy(
        both_ref.at[1 - half], other_ref, send_sem, recv_sem,
        device_id=sibling, device_id_type=MESH,
    )
    away.start()
    away.wait()


def swap_pair(both):
    return pl.pallas_call(
        swap_pair_kernel,
        name="swap_pair",
        out_shape=jax.ShapeDtypeStruct(both.shape[1:], both.dtype),
        in_specs=[pl.BlockSpec(memory_space=pl.ANY)],
        out_specs=pl.BlockSpec(memory_space=pl.ANY),
        scratch_shapes=[pltpu.SemaphoreType.DMA(())] * 2,
        compiler_params=params_of(2),
    )(both)


def places():
    dp, rank = lax.axis_index("dp"), lax.axis_index("tensor")
    core, y = lax.rem(rank, 2), rank // 2
    z, x = dp // 2, lax.rem(dp, 2)
    sibling = {"dp": dp, "tensor": rank + 1 - 2 * core}
    near_x = {"dp": dp + 1 - 2 * x, "tensor": rank}
    near_y = {"dp": dp, "tensor": rank + 2 - 4 * y}
    first = {"dp": dp + (1 - core) * (1 - 2 * x), "tensor": rank + core * (2 - 4 * y)}
    second = {"dp": dp + core * (1 - 2 * x), "tensor": rank + (1 - core) * (2 - 4 * y)}
    xa, ya = x + (1 - core) * (1 - 2 * x), y + core * (1 - 2 * y)
    xb, yb = x + core * (1 - 2 * x), y + (1 - core) * (1 - 2 * y)
    return dict(dp=dp, rank=rank, core=core, y=y, z=z, x=x, sibling=sibling, first=first, second=second,
                xa=xa, ya=ya, xb=xb, yb=yb)


def line_jumps(dp, rank, z, n):
    jumps, hop = [], 1
    while hop < n:
        bit = lax.rem(z // hop, 2)
        jumps.append({"dp": dp + 2 * hop * (1 - 2 * bit), "tensor": rank})
        hop *= 2
    return jumps


def start_kernel(
    n, mine_ref, vec_ref, x_ref, w_hbm, qkv_hbm, other_hbm, vec_out,
    out_ref, chip, sib, qkv, vec_sent, vec_got,
    local_sem, pair_sem, zs, zr, as_, ar, bs, br, ss, sr, ks, kr, vs, vr,
):
    w = places()
    dp, rank, core, y, z, x = (w[k] for k in ("dp", "rank", "core", "y", "z", "x"))
    block, wide = mine_ref.shape[1], mine_ref.shape[2]
    slab = block // 2
    up, down = {"dp": lax.rem(dp + 2, 2 * n), "tensor": rank}, {"dp": lax.rem(dp + 2 * n - 2, 2 * n), "tensor": rank}
    partners = [w["sibling"], w["second"], w["first"]] + line_jumps(dp, rank, z, n)
    meet([up, down] + partners)

    pair = pltpu.make_async_remote_copy(mine_ref, sib, pair_sem.at[0], pair_sem.at[1], device_id=w["sibling"], device_id_type=MESH)
    pair.start()

    def small_send(step):
        return pltpu.make_async_remote_copy(vec_sent.at[step], vec_got.at[step], vs.at[step], vr.at[step], device_id=partners[step], device_id_type=MESH)

    def small_step(step):
        small_send(step).wait_recv()
        vec_sent[step + 1] = vec_sent[step] + vec_got[step]
        if step + 1 < len(partners):
            small_send(step + 1).start()

    vec_sent[0] = vec_ref[...]
    small_send(0).start()
    pair.wait()
    chip[...] = mine_ref[...] + sib[...]
    rows_own = pl.ds(pl.multiple_of(core * slab, slab), slab)
    own_at = pl.ds(pl.multiple_of(dp * block, block), block)
    cols_own = pl.ds(pl.multiple_of(y * wide, wide), wide)
    keep = pltpu.make_async_copy(chip, out_ref.at[:, own_at, cols_own], local_sem.at[0])
    keep.start()

    def spot(g, zi, xi, yi):
        d = zi * 2 + xi
        rows = pl.ds(pl.multiple_of(d * block + core * slab, slab), slab)
        cols = pl.ds(pl.multiple_of(yi * wide, wide), wide)
        return out_ref.at[:, rows, cols]

    def own(g):
        return chip.at[:, rows_own, :]

    def move(g, zi, xi, yi, dev, ssem, rsem, source=None):
        at = spot(g, zi, xi, yi)
        return pltpu.make_async_remote_copy(at if source is None else source, at, ssem, rsem, device_id=dev, device_id_type=MESH)

    def line_up(g, s):
        return move(g, z - s, x, y, up, zs.at[g, 0, s], zr.at[g, 0, s], own(g) if s == 0 else None)

    def line_down(g, s):
        return move(g, z + s, x, y, down, zs.at[g, 1, s], zr.at[g, 1, s], own(g) if s == 0 else None)

    def to_first(g, zi, source=None):
        return move(g, zi, x, y, w["first"], as_.at[g, zi], ar.at[g, zi], source)

    def to_second(g, zi, far, source=None):
        xi, yi = (w["xa"], w["ya"]) if far else (x, y)
        return move(g, zi, xi, yi, w["second"], bs.at[g, far, zi], br.at[g, far, zi], source)

    def to_sibling(g, zi, quarter, source=None):
        xi = (x, w["xa"], w["xb"], w["xa"] + w["xb"] - x)[quarter]
        yi = (y, w["ya"], w["yb"], w["ya"] + w["yb"] - y)[quarter]
        return move(g, zi, xi, yi, w["sibling"], ss.at[g, quarter, zi], sr.at[g, quarter, zi], source)

    def begin(g):
        @pl.when(z < n - 1)
        def _():
            line_up(g, 0).start()

        @pl.when(z > 0)
        def _():
            line_down(g, 0).start()

        to_first(g, z, own(g)).start()
        to_second(g, z, 0, own(g)).start()

    def first_in(g, zi):
        got = move(g, zi, w["xa"], w["ya"], w["first"], as_.at[g, zi], ar.at[g, zi])
        got.wait_recv()
        to_second(g, zi, 1).start()
        to_sibling(g, zi, 1).start()

    def second_in(g, zi, far):
        q = 2 + far
        xi = (w["xb"], w["xa"] + w["xb"] - x)[far]
        yi = (w["yb"], w["ya"] + w["yb"] - y)[far]
        move(g, zi, xi, yi, w["second"], bs.at[g, far, zi], br.at[g, far, zi]).wait_recv()
        to_sibling(g, zi, q).start()

    def below_in(g, s):
        zi = z - 1 - s
        move(g, zi, x, y, up, zs.at[g, 0, s], zr.at[g, 0, s]).wait_recv()
        if s + 1 < n - 1:
            @pl.when(z < n - 1)
            def _():
                line_up(g, s + 1).start()
        to_first(g, zi).start()
        to_second(g, zi, 0).start()
        to_sibling(g, zi, 0).start()

    def above_in(g, s):
        zi = z + 1 + s
        move(g, zi, x, y, down, zs.at[g, 1, s], zr.at[g, 1, s]).wait_recv()
        if s + 1 < n - 1:
            @pl.when(z > 0)
            def _():
                line_down(g, s + 1).start()
        to_first(g, zi).start()
        to_second(g, zi, 0).start()
        to_sibling(g, zi, 0).start()

    def steps(gs):
        for g in gs:
            first_in(g, z)
        for s in range(n - 1):
            @pl.when(z - 1 - s >= 0)
            def _(s=s):
                for g in gs:
                    below_in(g, s)

            @pl.when(z + 1 + s < n)
            def _(s=s):
                for g in gs:
                    above_in(g, s)
            if s > 0:
                both(s, lambda g, zi: first_in(g, zi), gs)
        both(n - 1, lambda g, zi: first_in(g, zi), gs)
        for g in gs:
            second_in(g, z, 0)
        for g in gs:
            second_in(g, z, 1)
        for s in range(1, n):
            both(s, lambda g, zi: second_in(g, zi, 0), gs)
            both(s, lambda g, zi: second_in(g, zi, 1), gs)

    def both(s, what, gs):
        @pl.when(z - s >= 0)
        def _():
            for g in gs:
                what(g, z - s)

        @pl.when(z + s < n)
        def _():
            for g in gs:
                what(g, z + s)

    begin(0)
    small_step(0)
    steps((0,))
    for step in range(1, len(partners)):
        small_step(step)

    keep.wait()
    for zi in range(n):
        for q in range(1, 4):
            to_sibling(0, zi, q).wait_recv()

        @pl.when(zi != z)
        def _(zi=zi):
            to_sibling(0, zi, 0).wait_recv()
    save_w = pltpu.make_async_copy(out_ref, w_hbm, local_sem.at[1])
    save_w.start()

    rows, width = x_ref.shape
    third = width // 2
    vec_out[...] = vec_sent[len(partners)]
    tiles = rows // ROWS

    def keys_of(t, yi):
        at = (pl.ds(pl.multiple_of(t * ROWS, ROWS), ROWS), slice((3 * yi + 1) * third, (3 * yi + 3) * third))
        far = (at[0], slice(2 * yi * third, 2 * (yi + 1) * third))
        return pltpu.make_async_remote_copy(qkv.at[at], other_hbm.at[far], ks.at[t, yi], kr.at[t, yi], device_id=w["sibling"], device_id_type=MESH)

    @pl.loop(0, tiles)
    def _(t):
        at = pl.ds(pl.multiple_of(t * ROWS, ROWS), ROWS)
        for yi in range(2):
            both = nn(x_ref[at, :], out_ref[0, :, yi * wide + third : yi * wide + 3 * third])
            first = (3 * yi + 1) * third
            qkv[at, first : first + third] = both[:, :third].astype(BF)
            bias = vec_out[1:2, yi * third : (yi + 1) * third]
            qkv[at, first + third : first + 2 * third] = (both[:, third:] + bias).astype(BF)
            keys_of(t, yi).start()

    @pl.loop(0, tiles)
    def _(t):
        at = pl.ds(pl.multiple_of(t * ROWS, ROWS), ROWS)
        for yi in range(2):
            bias = vec_out[0:1, yi * third : (yi + 1) * third]
            mine = nn(x_ref[at, :], out_ref[0, :, yi * wide : yi * wide + third]) + bias
            qkv[at, 3 * yi * third : (3 * yi + 1) * third] = mine.astype(BF)

    save_qkv = pltpu.make_async_copy(qkv, qkv_hbm, local_sem.at[2])
    save_qkv.start()
    for g in (0,):
        @pl.when(z < n - 1)
        def _(g=g):
            line_up(g, 0).wait_send()

        @pl.when(z > 0)
        def _(g=g):
            line_down(g, 0).wait_send()
        for s in range(1, n - 1):
            @pl.when((z < n - 1) & (z - s >= 0))
            def _(g=g, s=s):
                line_up(g, s).wait_send()

            @pl.when((z > 0) & (z + s < n))
            def _(g=g, s=s):
                line_down(g, s).wait_send()
        for zi in range(n):
            to_first(g, zi).wait_send()
            for far in range(2):
                to_second(g, zi, far).wait_send()
            for q in range(1, 4):
                to_sibling(g, zi, q).wait_send()
        for zi in range(n):
            @pl.when(zi != z)
            def _(g=g, zi=zi):
                to_sibling(g, zi, 0).wait_send()


    for step in range(len(partners)):
        small_send(step).wait_send()

    @pl.loop(0, tiles)
    def _(t):
        for yi in range(2):
            keys_of(t, yi).wait()
    save_w.wait()
    save_qkv.wait()


def start(mine, vec, layer_in):
    dp, tp = lax.axis_size("dp"), lax.axis_size("tensor")
    n = dp // 2
    parts, block, wide = mine.shape
    rows, width = layer_in.shape
    steps = 3 + (n - 1).bit_length()
    tiles = rows // ROWS
    dma = pltpu.SemaphoreType.DMA
    anywhere, inside = pl.BlockSpec(memory_space=pl.ANY), pl.BlockSpec(memory_space=pltpu.VMEM)
    whole = (parts, dp * block, wide * tp // 2)
    return pl.pallas_call(
        partial(start_kernel, n),
        name="start",
        in_specs=[inside] * 3,
        out_specs=[anywhere] * 3 + [inside],
        out_shape=[
            jax.ShapeDtypeStruct(whole, BF),
            jax.ShapeDtypeStruct((rows, 3 * width), BF),
            jax.ShapeDtypeStruct((rows, 2 * width), BF),
            jax.ShapeDtypeStruct(vec.shape, F32),
        ],
        scratch_shapes=[
            pltpu.VMEM(whole, BF), pltpu.VMEM(mine.shape, BF), pltpu.VMEM(mine.shape, BF),
            pltpu.VMEM((rows, 3 * width), BF),
            pltpu.VMEM((steps + 1,) + vec.shape, F32), pltpu.VMEM((steps,) + vec.shape, F32),
            dma((3,)), dma((2,)), dma((1, 2, n)), dma((1, 2, n)), dma((1, n)), dma((1, n)),
            dma((1, 2, n)), dma((1, 2, n)), dma((1, 4, n)), dma((1, 4, n)), dma((tiles, 2)), dma((tiles, 2)),
            dma((steps,)), dma((steps,)),
        ],
        compiler_params=params_of(3),
    )(mine, vec, layer_in)


def in_tiles(block):
    return block % 32 == 0


def start_plainly(mine, vec, layer_in):
    dp, tp = lax.axis_size("dp"), lax.axis_size("tensor")
    parts, block, wide = mine.shape
    width = layer_in.shape[1]
    third = width // 2
    every = lax.all_gather(mine, ("dp", "tensor"), axis=0, tiled=False)
    every = every.reshape(dp, tp // 2, 2, parts, block, wide).sum(axis=2)
    weights = every.transpose(2, 0, 3, 1, 4).reshape(parts, dp * block, tp // 2 * wide)
    vec = lax.psum(vec, ("dp", "tensor"))
    zero = jnp.zeros((1, third), F32)
    bias = jnp.concatenate(
        [v for y in range(2) for v in (vec[:1, y * third : (y + 1) * third], zero,
                                       vec[1:2, y * third : (y + 1) * third])], axis=1,
    )
    wqkv = weights[0].reshape(width, 2, 4 * third)[:, :, : 3 * third].reshape(width, 3 * width)
    qkv = (nn(layer_in, wqkv) + bias).astype(BF)
    return weights, qkv, swap_keys(qkv), vec


def q_lanes(p, pairs):
    third = pairs // 2 * PAIR
    first = p // (pairs // 2) * 3 * third + p % (pairs // 2) * PAIR
    return slice(first, first + PAIR)


def k_lanes(p, pairs):
    third = pairs // 2 * PAIR
    first = p // (pairs // 2) * 2 * third + p % (pairs // 2) * PAIR
    return slice(first, first + PAIR)


def v_lanes(p, pairs):
    third = pairs // 2 * PAIR
    lanes = k_lanes(p, pairs)
    return slice(lanes.start + third, lanes.stop + third)


def fetch_keys(qkv_ref, other_ref, kv, sems):
    rows, third = other_ref.shape[0], other_ref.shape[1] // 4
    half = lax.rem(lax.axis_index("tensor"), 2)
    here = pl.ds(pl.multiple_of(half * rows, rows), rows)
    there = pl.ds(pl.multiple_of((1 - half) * rows, rows), rows)
    moves = [pltpu.make_async_copy(other_ref, kv.at[there, :], sems.at[2])]
    for y in range(2):
        moves.append(
            pltpu.make_async_copy(
                qkv_ref.at[:, (3 * y + 1) * third : (3 * y + 3) * third],
                kv.at[here, 2 * y * third : 2 * (y + 1) * third],
                sems.at[y],
            )
        )
    for move in moves:
        move.start()
    for move in moves:
        move.wait()


def masked_pairs(source, target, lanes_of, pairs, scale):
    rows = source.shape[0]
    low_lanes = lax.broadcasted_iota(jnp.int32, (rows, PAIR), 1) < HD
    for p in range(pairs):
        both = source[:, lanes_of(p)]
        if scale is not None:
            both = both * jnp.asarray(scale, both.dtype)
        zero = jnp.zeros_like(both)
        target[p, :rows, :] = jnp.where(low_lanes, both, zero)
        target[p, rows:, :] = jnp.where(low_lanes, zero, both)


def tile_bias(j, q_first, row_info, key_info, bias):
    seg_q, bits_q = row_info[0:1, :], row_info[1:2, :]
    queries = bias.shape[1]
    for part in range(KT // HD):
        block = j * (KT // HD) + part
        bit = jnp.bitwise_and(
            lax.shift_right_logical(bits_q, jnp.full_like(bits_q, block)), 1
        )
        wanted = jnp.where(bit == 1, seg_q, -1)
        base = pl.multiple_of(j * KT + part * HD, HD)
        seg_k = key_info[pl.ds(base, HD), :]
        key_at = base + lax.broadcasted_iota(jnp.int32, (HD, queries), 0)
        query_at = q_first + lax.broadcasted_iota(jnp.int32, (HD, queries), 1)
        allowed = (seg_k == wanted) | (key_at == query_at)
        bias[part * HD : (part + 1) * HD, :] = jnp.where(allowed, 0.0, NEGATIVE)


def attend_forward_kernel(
    bounds, q_ref, qkv_ref, other_ref, row_info, key_info, out_ref, log_ref,
    q_pairs, kv_ref, v_turned, bias, top, total, acc, sems,
):
    step = pl.program_id(0)
    rows, width = out_ref.shape
    pairs = width // PAIR
    tiles = kv_ref.shape[0] // KT

    @pl.when(step == 0)
    def _():
        fetch_keys(qkv_ref, other_ref, kv_ref, sems)
        for j in range(tiles):
            for p in range(pairs):
                span = slice(p * PAIR, (p + 1) * PAIR)
                v_turned[j, span, :] = kv_ref[j * KT : (j + 1) * KT, v_lanes(p, pairs)].T

    masked_pairs(q_ref, q_pairs, partial(q_lanes, pairs=pairs), pairs, HD**-0.5)
    top[...] = jnp.full_like(top, NEGATIVE)
    total[...] = jnp.zeros_like(total)
    acc[...] = jnp.zeros_like(acc)
    q_first = bounds[step, 2]

    @pl.loop(bounds[step, 0], bounds[step, 1])
    def _(j):
        tile_bias(j, q_first, row_info, key_info, bias)
        keys_at = pl.multiple_of(j * KT, KT)
        for p in range(pairs):
            keys = kv_ref[pl.ds(keys_at, KT), k_lanes(p, pairs)]
            scores = nt(keys, q_pairs[p])
            for e in range(2):
                h = 2 * p + e
                mine = scores[:, e * rows : (e + 1) * rows] + bias[...]
                before = top[h : h + 1, :]
                now = jnp.maximum(before, jnp.max(mine, axis=0, keepdims=True))
                fade = jnp.exp(before - now)
                expos = jnp.exp(mine - now)
                top[h : h + 1, :] = now
                total[h : h + 1, :] = fade * total[h : h + 1, :] + jnp.sum(
                    expos, axis=0, keepdims=True
                )
                span = slice(h * HD, (h + 1) * HD)
                acc[span, :] = acc[span, :] * fade + nn(v_turned[j, span, :], expos.astype(BF))

    heads = width // HD
    for h in range(heads):
        span = slice(h * HD, (h + 1) * HD)
        acc[span, :] = acc[span, :] / total[h : h + 1, :]
    out_ref[...] = acc[...].T.astype(BF)
    log_ref[...] = top[...] + jnp.log(jnp.maximum(total[...], 1e-37))


def attend_forward(bounds, qkv, other, row_info, key_info):
    rows, width = qkv.shape[0], qkv.shape[1] // 3
    keys = 2 * rows
    stat_rows = 16
    return pl.pallas_call(
        attend_forward_kernel,
        name="attend_forward",
        grid_spec=pltpu.PrefetchScalarGridSpec(
            num_scalar_prefetch=1,
            grid=(rows // QT,),
            in_specs=[
                pl.BlockSpec((QT, 3 * width), lambda i, b: (i, 0)),
                pl.BlockSpec(memory_space=pl.ANY),
                pl.BlockSpec(memory_space=pl.ANY),
                pl.BlockSpec((8, QT), lambda i, b: (0, i)),
                pl.BlockSpec((keys, 1), lambda i, b: (0, 0), pipeline_mode=pl.Buffered(1)),
            ],
            out_specs=[
                pl.BlockSpec((QT, width), lambda i, b: (i, 0)),
                pl.BlockSpec((stat_rows, QT), lambda i, b: (0, i)),
            ],
            scratch_shapes=[
                pltpu.VMEM((width // PAIR, 2 * QT, PAIR), BF),
                pltpu.VMEM((keys, 2 * width), BF),
                pltpu.VMEM((keys // KT, width, KT), BF),
                pltpu.VMEM((KT, QT), F32),
                pltpu.VMEM((stat_rows, QT), F32),
                pltpu.VMEM((stat_rows, QT), F32),
                pltpu.VMEM((width, QT), F32),
                pltpu.SemaphoreType.DMA((3,)),
            ],
        ),
        out_shape=[
            jax.ShapeDtypeStruct((rows, width), BF),
            jax.ShapeDtypeStruct((stat_rows, rows), F32),
        ],
        compiler_params=params_of(),
    )(bounds, qkv, qkv, other, row_info, key_info)


def attend_backward_kernel(
    bounds, q_ref, qkv_ref, other_ref, row_info, key_info, out_ref, log_ref, grad_ref,
    dq_ref, dkv_ref, q_pairs, g_pairs, kv_ref, k_turned, bias, inner, dq_acc, dkv_acc, sems,
):
    step = pl.program_id(0)
    rows, width = out_ref.shape
    pairs = width // PAIR
    tiles = kv_ref.shape[0] // KT

    @pl.when(step == 0)
    def _():
        fetch_keys(qkv_ref, other_ref, kv_ref, sems)
        for j in range(tiles):
            for p in range(pairs):
                span = slice(p * PAIR, (p + 1) * PAIR)
                k_turned[j, span, :] = kv_ref[j * KT : (j + 1) * KT, k_lanes(p, pairs)].T
        dkv_acc[...] = jnp.zeros_like(dkv_acc)

    masked_pairs(q_ref, q_pairs, partial(q_lanes, pairs=pairs), pairs, HD**-0.5)
    masked_pairs(grad_ref, g_pairs, lambda p: slice(p * PAIR, (p + 1) * PAIR), pairs, None)
    head_of = lax.broadcasted_iota(jnp.int32, (inner.shape[0], width), 1) // HD
    row_of = lax.broadcasted_iota(jnp.int32, (inner.shape[0], width), 0)
    chosen = jnp.where(head_of == row_of, 1.0, 0.0)
    product = out_ref[...].astype(F32) * grad_ref[...].astype(F32)
    inner[...] = nt(chosen, product, precision=lax.Precision.HIGHEST)
    dq_acc[...] = jnp.zeros_like(dq_acc)
    q_first = bounds[step, 2]

    @pl.loop(bounds[step, 0], bounds[step, 1])
    def _(j):
        tile_bias(j, q_first, row_info, key_info, bias)
        here = pl.ds(pl.multiple_of(j * KT, KT), KT)
        for p in range(pairs):
            k_here, v_here = k_lanes(p, pairs), v_lanes(p, pairs)
            scores = nt(kv_ref[here, k_here], q_pairs[p])
            grad_probs = nt(kv_ref[here, v_here], g_pairs[p])
            probs, grads = [], []
            for e in range(2):
                h = 2 * p + e
                cols = slice(e * rows, (e + 1) * rows)
                prob = jnp.exp(scores[:, cols] + bias[...] - log_ref[h : h + 1, :])
                grad = (prob * (grad_probs[:, cols] - inner[h : h + 1, :])).astype(BF)
                probs.append(prob.astype(BF))
                grads.append(grad)
                span = slice(h * HD, (h + 1) * HD)
                dq_acc[span, :] += nn(k_turned[j, span, :], grad)
            dkv_acc[here, k_here] += nn(jnp.concatenate(grads, axis=1), q_pairs[p])
            dkv_acc[here, v_here] += nn(jnp.concatenate(probs, axis=1), g_pairs[p])

    dq_ref[...] = (dq_acc[...] * HD**-0.5).T.astype(BF)

    @pl.when(step == pl.num_programs(0) - 1)
    def _():
        dkv_ref[...] = dkv_acc[...].astype(BF)


def attend_backward(bounds, qkv, other, row_info, key_info, attn, logs, grad_attn):
    rows, width = attn.shape
    keys = 2 * rows
    stat_rows = logs.shape[0]
    whole = dict(pipeline_mode=pl.Buffered(1))
    return pl.pallas_call(
        attend_backward_kernel,
        name="attend_backward",
        grid_spec=pltpu.PrefetchScalarGridSpec(
            num_scalar_prefetch=1,
            grid=(rows // QT,),
            in_specs=[
                pl.BlockSpec((QT, 3 * width), lambda i, b: (i, 0)),
                pl.BlockSpec(memory_space=pl.ANY),
                pl.BlockSpec(memory_space=pl.ANY),
                pl.BlockSpec((8, QT), lambda i, b: (0, i)),
                pl.BlockSpec((keys, 1), lambda i, b: (0, 0), **whole),
                pl.BlockSpec((QT, width), lambda i, b: (i, 0)),
                pl.BlockSpec((stat_rows, QT), lambda i, b: (0, i)),
                pl.BlockSpec((QT, width), lambda i, b: (i, 0)),
            ],
            out_specs=[
                pl.BlockSpec((QT, width), lambda i, b: (i, 0)),
                pl.BlockSpec((keys, 2 * width), lambda i, b: (0, 0), **whole),
            ],
            scratch_shapes=[
                pltpu.VMEM((width // PAIR, 2 * QT, PAIR), BF),
                pltpu.VMEM((width // PAIR, 2 * QT, PAIR), BF),
                pltpu.VMEM((keys, 2 * width), BF),
                pltpu.VMEM((keys // KT, width, KT), BF),
                pltpu.VMEM((KT, QT), F32),
                pltpu.VMEM((stat_rows, QT), F32),
                pltpu.VMEM((width, QT), F32),
                pltpu.VMEM((keys, 2 * width), F32),
                pltpu.SemaphoreType.DMA((3,)),
            ],
        ),
        out_shape=[
            jax.ShapeDtypeStruct((rows, width), BF),
            jax.ShapeDtypeStruct((keys, 2 * width), BF),
        ],
        compiler_params=params_of(),
    )(bounds, qkv, qkv, other, row_info, key_info, attn, logs, grad_attn)


def attention_plan(segment_ids, pad_mask, random_blocks, global_blocks, rows):
    seq_count, nblocks = random_blocks.shape[0], random_blocks.shape[1]
    seq_len = segment_ids.shape[0] // seq_count
    rank = lax.axis_index("tensor")
    seq, half = rank // 2, lax.rem(rank, 2)
    segs = lax.dynamic_index_in_dim(segment_ids.reshape(seq_count, seq_len), seq, 0, False)
    pads = lax.dynamic_index_in_dim(pad_mask.reshape(seq_count, seq_len), seq, 0, False)
    randoms = lax.dynamic_index_in_dim(random_blocks, seq, 0, False)
    globs = lax.dynamic_index_in_dim(global_blocks, seq, 0, False)
    block_size = seq_len // nblocks
    one = jnp.int32(1)
    block = jnp.arange(nblocks, dtype=jnp.int32)

    def either(a, b):
        return jnp.bitwise_or(a, b)

    block_bits = lax.shift_left(one, block)
    window = either(
        block_bits,
        either(
            jnp.where(block > 0, lax.shift_left(one, jnp.maximum(block - 1, 0)), 0),
            jnp.where(
                block < nblocks - 1, lax.shift_left(one, jnp.minimum(block + 1, nblocks - 1)), 0
            ),
        ),
    )
    for r in range(randoms.shape[1]):
        window = either(window, lax.shift_left(one, randoms[:, r]))
    glob_bits = either(lax.shift_left(one, globs[:, 0]), lax.shift_left(one, globs[:, 1]))
    first = half * rows
    seg_q = lax.dynamic_slice_in_dim(segs, first, rows)
    own_bits = lax.dynamic_slice_in_dim(window, half * (rows // block_size), rows // block_size)
    bits = jnp.broadcast_to(own_bits[:, None], (rows // block_size, block_size)).reshape(rows)
    numbers = jnp.arange(globs.shape[0], dtype=jnp.int32)
    is_doc = seg_q[None, :] == numbers[:, None]
    bits = either(bits, jnp.sum(jnp.where(is_doc, glob_bits[:, None], 0), axis=0))
    row_info = jnp.concatenate(
        [seg_q[None], bits[None], jnp.zeros((6, rows), jnp.int32)], axis=0
    )
    key_info = jnp.where(pads == 1, segs, -2)[:, None]
    tiles = seg_q.reshape(rows // QT, QT)
    low = jnp.sum((segs[None, :] < tiles[:, :1]).astype(jnp.int32), axis=1)
    high = jnp.sum((segs[None, :] <= tiles[:, -1:]).astype(jnp.int32), axis=1)
    starts = first + QT * jnp.arange(rows // QT, dtype=jnp.int32)
    bounds = jnp.stack([low // KT, (high + KT - 1) // KT, starts, starts], axis=1)
    return bounds, row_info, key_info


TAIL_STEP = 0.47
TAIL = (0.266306628, 0.248031891, 0.336199252, -0.126105651, 0.607561554, -0.420410983, 0.0884173167)


def gelu_and_slope(pre):
    bell = jnp.exp(-0.5 * pre * pre)
    t = 1.0 / (1.0 + (TAIL_STEP * 0.5**0.5) * jnp.abs(pre))
    tail = TAIL[-1]
    for c in TAIL[-2::-1]:
        tail = tail * t + c
    tail = 0.5 * (tail * t) * bell
    cdf = jnp.where(pre < 0, tail, 1.0 - tail)
    return pre * cdf, cdf + pre * (bell * (2.0 * 3.141592653589793) ** -0.5)


def normalize(resid):
    center = resid - jnp.mean(resid, axis=1, keepdims=True)
    inverse = lax.rsqrt(jnp.mean(center * center, axis=1, keepdims=True) + EPSILON)
    return center * inverse, inverse


def norm_backward(grad_normed, normal_hat, inverse, gain):
    grad_hat = grad_normed * gain
    return inverse * (
        grad_hat
        - jnp.mean(grad_hat, axis=1, keepdims=True)
        - normal_hat * jnp.mean(grad_hat * normal_hat, axis=1, keepdims=True)
    )


def middle_kernel(
    x_ref, attn_ref, cot_ref, w_ref, blocks_ref, vec_ref,
    final_ref, first_grad, attn_grad, norm_low, unit_grad, proj_grad, out_grad,
    sums, unit_sums, slope, hidden, outer,
):
    width = x_ref.shape[1]
    third = width // 2
    wide = w_ref.shape[2] // 2
    proj_cols = [slice((y + 1) * wide - third, (y + 1) * wide) for y in range(2)]
    halves = [slice(y * third, (y + 1) * third) for y in range(2)]
    own_units = blocks_ref.shape[3] // 2
    chunks = [(t, slice(t * own_units, (t + 1) * own_units)) for t in range(blocks_ref.shape[1])]

    def w_in(t):
        return blocks_ref[:, t, :, :own_units].reshape(width, own_units)

    def w_out(t):
        return blocks_ref[:, t, :, own_units:].reshape(width, own_units)

    out_bias, last_bias, gain_1, shift_1, gain_2, shift_2 = (vec_ref[i : i + 1, :] for i in range(2, 8))

    @pl.when(pl.program_id(0) == 0)
    def _():
        sums[...] = jnp.zeros_like(sums)
        unit_sums[...] = jnp.zeros_like(unit_sums)
        outer[...] = jnp.zeros_like(outer)

    resid = x_ref[...].astype(F32) + out_bias
    for y in range(2):
        resid += nt(attn_ref[:, halves[y]], w_ref[0, :, proj_cols[y]])
    hat_1, inverse_1 = normalize(resid)
    first_norm = hat_1 * gain_1 + shift_1
    low = first_norm.astype(BF)
    norm_low[...] = low
    resid = first_norm + last_bias
    for t, cols in chunks:
        act, slope[:, cols] = gelu_and_slope(nn(low, w_in(t)) + vec_ref[8 + t : 9 + t, :own_units])
        act = act.astype(BF)
        hidden[:, cols] = act
        resid += nt(act, w_out(t))
    hat_2, inverse_2 = normalize(resid)
    final_ref[...] = (hat_2 * gain_2 + shift_2).astype(BF)

    cot = cot_ref[...].astype(F32)
    grad = norm_backward(cot, hat_2, inverse_2, gain_2)
    sums[6:7, :] += jnp.sum(cot * hat_2, axis=0, keepdims=True)
    sums[7:8, :] += jnp.sum(cot, axis=0, keepdims=True)
    sums[3:4, :] += jnp.sum(grad, axis=0, keepdims=True)
    low = grad.astype(BF)
    turned = low.T
    for t, cols in chunks:
        outer[t] += nn(turned, hidden[:, cols])
        act = (nn(low, w_out(t)) * slope[:, cols]).astype(BF)
        unit_grad[:, cols] = act
        unit_sums[0:1, cols] += jnp.sum(act.astype(F32), axis=0, keepdims=True)
        grad += nt(act, w_in(t))
    sums[4:5, :] += jnp.sum(grad * hat_1, axis=0, keepdims=True)
    sums[5:6, :] += jnp.sum(grad, axis=0, keepdims=True)
    grad = norm_backward(grad, hat_1, inverse_1, gain_1)
    sums[2:3, :] += jnp.sum(grad, axis=0, keepdims=True)
    first_grad[...] = grad
    low = grad.astype(BF)
    proj_grad[...] = low
    for y in range(2):
        attn_grad[:, halves[y]] = nn(low, w_ref[0, :, proj_cols[y]]).astype(BF)

    @pl.when(pl.program_id(0) == pl.num_programs(0) - 1)
    def _():
        for t, _ in chunks:
            out_grad[:, t] = outer[t].reshape(out_grad.shape[0], out_grad.shape[2], own_units).astype(BF)


def middle(layer_in, attn, output_grad, weights, blocks, vectors):
    rows, width = layer_in.shape
    units = blocks.shape[1] * blocks.shape[3] // 2
    tile = lambda w: pl.BlockSpec((ROWS, w), lambda i: (i, 0))
    whole = lambda a: pl.BlockSpec(a.shape, lambda i: (0,) * len(a.shape), pipeline_mode=pl.Buffered(1))
    fixed = lambda w: pl.BlockSpec((8, w), lambda i: (0, 0))
    shape = lambda w, t: jax.ShapeDtypeStruct((rows, w), t)
    out_grad = jax.ShapeDtypeStruct(blocks.shape[:3] + (blocks.shape[3] // 2,), BF)
    out_spec = pl.BlockSpec(out_grad.shape, lambda i: (0, 0, 0, 0), pipeline_mode=pl.Buffered(1))
    return pl.pallas_call(
        middle_kernel,
        name="middle",
        grid=(rows // ROWS,),
        in_specs=[tile(width)] * 3 + [whole(weights), whole(blocks), whole(vectors)],
        out_specs=[tile(width)] * 4 + [tile(units), tile(width), out_spec, fixed(width), fixed(units)],
        out_shape=[
            shape(width, BF), shape(width, F32), shape(width, BF), shape(width, BF), shape(units, BF), shape(width, BF),
            out_grad,
            jax.ShapeDtypeStruct((8, width), F32), jax.ShapeDtypeStruct((8, units), F32),
        ],
        scratch_shapes=[
            pltpu.VMEM((ROWS, units), F32),
            pltpu.VMEM((ROWS, units), BF),
            pltpu.VMEM((blocks.shape[1], width, units // blocks.shape[1]), F32),
        ],
        compiler_params=params_of(),
    )(layer_in, attn, output_grad, weights, blocks, vectors)


def finish_kernel(
    n, x_hbm, dq_hbm, dkv_hbm, w_hbm, first_hbm, low_hbm, unit_hbm, proj_hbm, attn_hbm, sums_ref, unit_sums,
    input_hbm, q_out, k_out, v_out, o_out, in_out, vec_out,
    rows_in, turned, unit, d_qkv, attn, far, w_all, tile_in, tile_out, grads, sib, from_b, from_a, from_low, from_high,
    result, vec_sent, vec_got,
    load, swap_s, swap_r, ss, sr, bs, br, as_, ar, zs, zr, es, er, vs, vr, tile_sem,
):
    w = places()
    dp, rank, core, y, z, x = (w[k] for k in ("dp", "rank", "core", "y", "z", "x"))
    rows, width = x_hbm.shape
    third = width // 2
    wide = unit.shape[1] // 2
    slab = result.shape[1] // 2
    up, down = {"dp": lax.rem(dp + 2, 2 * n), "tensor": rank}, {"dp": lax.rem(dp + 2 * n - 2, 2 * n), "tensor": rank}
    partners = [w["sibling"], w["second"], w["first"]] + line_jumps(dp, rank, z, n)
    barrier = pltpu.get_barrier_semaphore()
    for other in partners + [up, down]:
        pl.semaphore_signal(barrier, inc=1, device_id=other, device_id_type=MESH)

    def fetch(i, src, dst):
        return pltpu.make_async_copy(src, dst, load.at[i])

    fetch_low = fetch(0, low_hbm, rows_in.at[0])
    fetch_unit = fetch(1, unit_hbm, unit)
    fetch_x = fetch(2, x_hbm, rows_in.at[1])
    fetch_proj = fetch(3, proj_hbm, rows_in.at[2])
    fetch_attn = fetch(4, attn_hbm, attn)
    fetch_w = fetch(5, w_hbm.at[0], w_all)
    fetch_dq = [fetch(6 + h, dq_hbm.at[:, h * third : (h + 1) * third], d_qkv.at[:, 3 * h * third : (3 * h + 1) * third]) for h in range(2)]
    fetch_kv = [fetch(8 + h, dkv_hbm.at[core, :, 2 * h * third : 2 * (h + 1) * third], d_qkv.at[:, (3 * h + 1) * third : (3 * h + 3) * third]) for h in range(2)]
    for move in [fetch_low, fetch_unit, fetch_x, fetch_proj, fetch_attn] + fetch_dq + fetch_kv + [fetch_w]:
        move.start()
    pl.semaphore_wait(barrier, len(partners) + 2)

    def copy(src, dst, ssem, rsem, dev):
        return pltpu.make_async_remote_copy(src, dst, ssem, rsem, device_id=dev, device_id_type=MESH)

    swap = copy(dkv_hbm.at[1 - core], far, swap_s, swap_r, w["sibling"])
    swap.start()

    def turn_rows(i):
        for c in range(0, width, 128):
            turned[i, c : c + 128, :] = rows_in[i, :, c : c + 128].T

    places_of = [xd * 2 + yd for xd, yd in (
        (x, y), (w["xa"], w["ya"]), (w["xb"], w["yb"]), (w["xa"] + w["xb"] - x, w["ya"] + w["yb"] - y))]
    mine = grads.at[core]

    def keep(k, zd, yd, lane, value):
        for xd in range(2):
            for c in range(2):
                first = (xd * 2 + c) * slab
                grads[c, k, zd, xd * 2 + yd, :, lane : lane + value.shape[1]] = value[first : first + slab, :].astype(BF)

    def rows_of_line(i, zd):
        return turned[i, pl.ds(pl.multiple_of(zd * 4 * slab, 4 * slab), 4 * slab), :]

    def compute_inner(zd):
        left = rows_of_line(0, zd)
        for yd in range(2):
            for lane in range(0, wide, 768):
                keep(1, zd, yd, lane, nn(left, unit[:, yd * wide + lane : yd * wide + lane + 768]))

    def compute_others(zd):
        left = rows_of_line(1, zd)
        for yd in range(2):
            for i in range(3):
                at = (3 * yd + i) * third
                keep(0, zd, yd, i * third, nn(left, d_qkv[:, at : at + third]))
        left = rows_of_line(2, zd)
        for yd in range(2):
            keep(0, zd, yd, 3 * third, nn(left, attn[:, yd * third : (yd + 1) * third]))

    def to_sibling(k, zd):
        return copy(grads.at[1 - core, k, zd], sib.at[k, zd], ss.at[k, zd], sr.at[k, zd], w["sibling"])

    def over_b(k, far_side, zd):
        place = places_of[2 + far_side]
        return copy(mine.at[k, zd, place], from_b.at[k, far_side, zd], bs.at[k, far_side, zd], br.at[k, far_side, zd], w["second"])

    def over_a(k, zd):
        return copy(mine.at[k, zd, places_of[1]], from_a.at[k, zd], as_.at[k, zd], ar.at[k, zd], w["first"])

    def over_up(k, zd):
        return copy(mine.at[k, zd, places_of[0]], from_low.at[k, zd], zs.at[k, zd], zr.at[0, k, zd], up)

    def over_down(k, zd):
        return copy(mine.at[k, zd, places_of[0]], from_high.at[k, zd], zs.at[k, zd], zr.at[1, k, zd], down)

    def put(q, k, zd, more):
        place = places_of[q]
        total = grads[core, k, zd, place].astype(F32) + sib[k, zd, place].astype(F32)
        for term in more:
            total = total + term[...].astype(F32)
        grads[core, k, zd, place] = total.astype(BF)

    def stage_b(k, zd):
        to_sibling(k, zd).wait_recv()
        for far_side in (1, 0):
            put(2 + far_side, k, zd, ())
            over_b(k, far_side, zd).start()

    def stage_a(k, zd):
        over_b(k, 1, zd).wait_recv()
        put(1, k, zd, (from_b.at[k, 1, zd],))
        over_a(k, zd).start()

    def stage_line(k, zd):
        over_b(k, 0, zd).wait_recv()
        over_a(k, zd).wait_recv()
        put(0, k, zd, (from_b.at[k, 0, zd], from_a.at[k, zd]))

        @pl.when((zd > z) & (z == 0))
        def _():
            over_up(k, zd).start()

        @pl.when((zd < z) & (z == n - 1))
        def _():
            over_down(k, zd).start()

    def grow(k, zd, term):
        place = places_of[0]
        grads[core, k, zd, place] = (grads[core, k, zd, place].astype(F32) + term[...].astype(F32)).astype(BF)

    def stage_hop(k, zd):
        @pl.when((zd > z) & (z > 0))
        def _():
            over_up(k, zd).wait_recv()
            grow(k, zd, from_low.at[k, zd])
            over_up(k, zd).start()

        @pl.when((zd < z) & (z < n - 1))
        def _():
            over_down(k, zd).wait_recv()
            grow(k, zd, from_high.at[k, zd])
            over_down(k, zd).start()

    def turn(i):
        below, above = z, n - 1 - z
        near = jnp.minimum(below, above)
        only = jnp.maximum(below, above) - near
        side = jnp.where(above >= below, 1, -1)
        distance = jnp.where(i < only, only + near - i, near - (i - only) // 2)
        sign = jnp.where(i < only, side, jnp.where(lax.rem(i - only, 2) == 0, side, -side))
        return jnp.where(i == n - 1, z, z + sign * distance)

    def item(j):
        return 1 - j // n, turn(lax.rem(j, n))

    def small_send(step):
        return copy(vec_sent.at[step], vec_got.at[step], vs.at[step], vr.at[step], partners[step])

    def input_tile(t):
        at = pl.ds(pl.multiple_of(t * ROWS, ROWS), ROWS)
        return (pltpu.make_async_copy(first_hbm.at[at, :], tile_in.at[lax.rem(t, 2)], tile_sem.at[0, lax.rem(t, 2)]),
                pltpu.make_async_copy(tile_out.at[lax.rem(t, 2)], input_hbm.at[at, :], tile_sem.at[1, lax.rem(t, 2)]), at)

    def input_grad(t):
        into, out, at = input_tile(t)
        into.start()
        total = nt(d_qkv[at, : 3 * third], w_all[:, : 3 * third])
        total += nt(d_qkv[at, 3 * third :], w_all[:, wide : wide + 3 * third])
        into.wait()
        tile_out[lax.rem(t, 2)] = tile_in[lax.rem(t, 2)] + total
        out.start()

    tiles = rows // ROWS
    last_item = 2 * n

    fetch_low.wait()
    turn_rows(0)
    fetch_unit.wait()

    @pl.loop(0, last_item + 4)
    def _(j):
        @pl.when(j < n)
        def _():
            k, zd = item(j)
            compute_inner(zd)
            to_sibling(1, zd).start()

        @pl.when(j == n - 1)
        def _():
            fetch_x.wait()
            fetch_proj.wait()
            fetch_attn.wait()
            turn_rows(1)
            turn_rows(2)
            for move in fetch_dq + fetch_kv:
                move.wait()
            swap.wait_recv()
            for h in range(2):
                at = slice((3 * h + 1) * third, (3 * h + 3) * third)
                d_qkv[:, at] = (d_qkv[:, at].astype(F32) + far[:, 2 * h * third : 2 * (h + 1) * third].astype(F32)).astype(BF)
            vec_sent[0] = jnp.zeros_like(vec_sent[0])
            vec_sent[0, 2:8, :] = sums_ref[2:8, :]
            for h in range(2):
                for row, i in ((0, 0), (1, 2)):
                    cols = d_qkv[:, (3 * h + i) * third : (3 * h + i + 1) * third].astype(F32)
                    vec_sent[0, row : row + 1, h * third : (h + 1) * third] = jnp.sum(cols, axis=0, keepdims=True)
            for u in range(unit_sums.shape[1] // width):
                vec_sent[0, 8 + u : 9 + u, :] = unit_sums[0:1, u * width : (u + 1) * width]
            small_send(0).start()
            fetch_w.wait()

        @pl.when((j >= n) & (j < last_item))
        def _():
            k, zd = item(j)
            compute_others(zd)
            to_sibling(0, zd).start()

        @pl.when((j >= 1) & (j < last_item + 1))
        def _():
            stage_b(*item(j - 1))

        @pl.when((j >= 2) & (j < last_item + 2))
        def _():
            stage_a(*item(j - 2))

        @pl.when((j >= 3) & (j < last_item + 3))
        def _():
            stage_line(*item(j - 3))

        @pl.when(j >= 4)
        def _():
            stage_hop(*item(j - 4))

        for step in range(len(partners)):
            @pl.when(j == n + step)
            def _(step=step):
                small_send(step).wait_recv()
                vec_sent[step + 1] = vec_sent[step] + vec_got[step]
                if step + 1 < len(partners):
                    small_send(step + 1).start()

        @pl.when((j >= last_item - tiles) & (j < last_item))
        def _():
            t = j - (last_item - tiles)

            @pl.when(t >= 2)
            def _():
                input_tile(t - 2)[1].wait()
            input_grad(t)

    vec_out[...] = vec_sent[len(partners)]
    own = pl.ds(pl.multiple_of(core * slab, slab), slab)
    theirs = pl.ds(pl.multiple_of((1 - core) * slab, slab), slab)
    for k in (1, 0):
        result[k, own, :] = grads[core, k, z, places_of[0]].astype(F32)

        @pl.when(z > 0)
        def _():
            over_up(k, z).wait_recv()
            result[k, own, :] += from_low[k, z].astype(F32)

        @pl.when(z < n - 1)
        def _():
            over_down(k, z).wait_recv()
            result[k, own, :] += from_high[k, z].astype(F32)

        copy(result.at[k, own, :], result.at[k, own, :], es.at[k], er.at[k], w["sibling"]).start()
    for t in range(max(tiles - 2, 0), tiles):
        input_tile(t)[1].wait()
    swap.wait_send()
    for step in range(len(partners)):
        small_send(step).wait_send()

    @pl.loop(0, n)
    def _(zd):
        for k in range(2):
            to_sibling(k, zd).wait_send()
            over_b(k, 0, zd).wait_send()
            over_b(k, 1, zd).wait_send()
            over_a(k, zd).wait_send()

            @pl.when(zd > z)
            def _():
                over_up(k, zd).wait_send()

            @pl.when(zd < z)
            def _():
                over_down(k, zd).wait_send()
    for k in (1, 0):
        copy(result.at[k, theirs, :], result.at[k, theirs, :], es.at[k], er.at[k], w["sibling"]).wait()

    def chosen(k, lane, w_own):
        both = result[k, :, lane : lane + 2 * w_own]
        return jnp.where(core == 0, both[:, :w_own], both[:, w_own:])

    for i, out in enumerate((q_out, k_out, v_out, o_out)):
        out[...] = chosen(0, i * third, third // 2)
    in_out[...] = chosen(1, 0, wide // 2)


def finish(layer_in, dq, dkv, weights, grad_first, norm_low, unit_grad, proj_grad, attn, sums, unit_sums):
    rows, width = layer_in.shape
    units = unit_grad.shape[1]
    dp, tp = lax.axis_size("dp"), lax.axis_size("tensor")
    n = dp // 2
    block = width // dp
    slab, wide, third = block // 2, units // 2, width // 2
    steps = 3 + (n - 1).bit_length()
    dma = pltpu.SemaphoreType.DMA
    slabs = lambda *lead: pltpu.VMEM(lead + (slab, wide), BF)
    anywhere, inside = pl.BlockSpec(memory_space=pl.ANY), pl.BlockSpec(memory_space=pltpu.VMEM)
    result = lambda *shape: jax.ShapeDtypeStruct(shape, F32)
    return pl.pallas_call(
        partial(finish_kernel, n),
        name="finish",
        in_specs=[anywhere] * 9 + [inside] * 2,
        out_specs=[anywhere] + [inside] * 6,
        out_shape=[result(rows, width)] + [result(block, third // 2)] * 4 + [result(block, wide // 2), result(16, width)],
        scratch_shapes=[
            pltpu.VMEM((3, rows, width), BF),
            pltpu.VMEM((3, width, rows), BF),
            pltpu.VMEM((rows, units), BF),
            pltpu.VMEM((rows, 3 * width), BF),
            pltpu.VMEM((rows, width), BF),
            pltpu.VMEM((rows, 2 * width), BF),
            pltpu.VMEM((width, units), BF),
            pltpu.VMEM((2, ROWS, width), F32),
            pltpu.VMEM((2, ROWS, width), F32),
            slabs(2, 2, n, 4),
            slabs(2, n, 4),
            slabs(2, 2, n),
            slabs(2, n),
            slabs(2, n),
            slabs(2, n),
            pltpu.VMEM((2, block, wide), F32),
            pltpu.VMEM((steps + 1, 16, width), F32),
            pltpu.VMEM((steps, 16, width), F32),
            dma((10,)), dma(()), dma(()),
            dma((2, n)), dma((2, n)), dma((2, 2, n)), dma((2, 2, n)), dma((2, n)), dma((2, n)),
            dma((2, n)), dma((2, 2, n)), dma((2,)), dma((2,)), dma((steps,)), dma((steps,)), dma((2, 2)),
        ],
        compiler_params=pltpu.CompilerParams(
            collective_id=4, has_side_effects=True, vmem_limit_bytes=60 * 2**20
        ),
    )(layer_in, dq, dkv.reshape(2, rows, 2 * width), weights, grad_first, norm_low, unit_grad, proj_grad, attn, sums, unit_sums)


def finish_plainly(layer_in, dq, dkv, weights, grad_first, norm_low, unit_grad, proj_grad, attn, sums, unit_sums):
    rows, width = layer_in.shape
    units = unit_grad.shape[1]
    dp, tp = lax.axis_size("dp"), lax.axis_size("tensor")
    third, block, pairs = width // 2, width // dp, tp // 2
    half = lax.rem(lax.axis_index("tensor"), 2)
    both = dkv.reshape(2, rows, 2 * width)
    far = swap_pair(both)
    near = lax.dynamic_index_in_dim(both, half, 0, False)
    own = (near.astype(F32) + far.astype(F32)).astype(BF)
    d_qkv = jnp.concatenate([dq[:, :third], own[:, :width], dq[:, third:], own[:, width:]], axis=1)
    wqkv = weights[0].reshape(width, 2, 4 * third)[:, :, : 3 * third].reshape(width, 3 * width)
    input_grad = grad_first + nt(d_qkv, wqkv)
    grads = [g.astype(BF) for g in (tn(layer_in, d_qkv), tn(proj_grad, attn), tn(norm_low, unit_grad))]
    joined = jnp.concatenate([g.reshape(width, pairs, -1) for g in grads[:2]], axis=2)
    every = jnp.stack([joined.reshape(width, units), grads[2]])
    every = every.reshape(2, dp, block, pairs, 1, units // pairs).transpose(1, 3, 4, 0, 2, 5)
    every = jnp.broadcast_to(every, (dp, pairs, 2, 2, block, units // pairs))
    total = lax.psum_scatter(
        every.reshape(dp * tp, 2, block, units // pairs), ("dp", "tensor"), scatter_dimension=0, tiled=False
    ).astype(F32)
    d_bias = jnp.sum(d_qkv.astype(F32), axis=0).reshape(2, 3, third)
    vec = jnp.concatenate(
        [d_bias[:, 0].reshape(1, width), d_bias[:, 2].reshape(1, width), sums[2:],
         unit_sums[0].reshape(-1, width), jnp.zeros((8 - units // width, width), F32)], axis=0,
    )
    vec = lax.psum(vec, ("dp", "tensor"))

    def chosen(k, lane, w_own):
        return lax.dynamic_slice_in_dim(total[k], lane + half * w_own, w_own, axis=1)

    return (input_grad,) + tuple(chosen(0, i * third, third // 2) for i in range(4)) + (
        chosen(1, 0, units // tp), vec)


def on_device(
    layer_in, query_weight, key_weight, value_weight, output_weight, inner_weight, outer_weight,
    query_bias, value_bias, output_bias, inner_bias, outer_bias, first_gain, first_shift,
    second_gain, second_shift, segment_ids, pad_mask, random_blocks, global_blocks, output_grad,
):
    rows, width = layer_in.shape
    dp, tp = lax.axis_size("dp"), lax.axis_size("tensor")
    own_rows, own_cols = query_weight.shape
    own_units = inner_weight.shape[1]
    third = width // 2
    half = lax.rem(lax.axis_index("tensor"), 2)

    def beside(own):
        zero = jnp.zeros_like(own)
        return jnp.concatenate(
            [jnp.where(half == 0, own, zero), jnp.where(half == 0, zero, own)], axis=1
        )

    units_own = jnp.concatenate([inner_weight, outer_weight.T], axis=1)
    blocks = lax.all_gather(units_own, ("dp", "tensor"), axis=0, tiled=False)
    blocks = blocks.reshape(dp, tp, own_rows, 2 * own_units)
    mine = jnp.concatenate(
        [beside(w) for w in (query_weight, key_weight, value_weight, output_weight.T)], axis=1
    )[None]
    place = lax.axis_index("dp") * tp + lax.axis_index("tensor")
    one, own_bias = query_bias.shape[0], inner_bias.shape[0]
    small = jnp.stack([query_bias, value_bias, output_bias, outer_bias, first_gain, first_shift,
                       second_gain, second_shift])
    eight = lax.dynamic_update_slice(jnp.zeros((8, width), F32), small, (0, place * one))
    unit = lax.dynamic_update_slice(jnp.zeros((8 * width,), F32), inner_bias, (place * own_bias,))
    vec = jnp.concatenate([eight, unit.reshape(8, width)], axis=0)
    begin = start if in_tiles(own_rows) else start_plainly
    weights, qkv, other, vectors = begin(mine, vec, layer_in)

    bounds, row_info, key_info = attention_plan(
        segment_ids, pad_mask, random_blocks, global_blocks, rows
    )
    attn, logs = attend_forward(bounds, qkv, other, row_info, key_info)
    (layer_out, grad_first, grad_attn, norm_low, unit_grad, proj_grad, out_grad, sums, unit_sums) = middle(
        layer_in, attn, output_grad, weights, blocks, vectors
    )
    d_outer = lax.psum_scatter(
        out_grad.reshape((dp * tp,) + out_grad.shape[2:]), ("dp", "tensor"), scatter_dimension=0, tiled=False
    )
    dq, dkv = attend_backward(bounds, qkv, other, row_info, key_info, attn, logs, grad_attn)
    end = finish if in_tiles(own_rows) else finish_plainly
    input_grad, d_q, d_k, d_v, d_o, d_inner, vec = end(
        layer_in, dq, dkv, weights, grad_first, norm_low, unit_grad, proj_grad, attn, sums, unit_sums
    )
    pieces = lax.dynamic_slice_in_dim(vec[:8], place * one, one, axis=1)
    (r_bq, r_bv, r_bo, r_bout, r_g1, r_s1, r_g2, r_s2) = (pieces[i] for i in range(8))
    d_bin = lax.dynamic_slice_in_dim(vec[8:].reshape(-1), place * own_bias, own_bias)
    return (
        layer_out, input_grad, d_q, d_k, d_v, d_o.T, d_inner, d_outer.astype(F32).T,
        r_bq, r_bv, r_bo, d_bin, r_bout, r_g1, r_s1, r_g2, r_s2,
    )


def solution(mesh):
    tokens = P(("dp", "tensor"), None)
    vector = P(("dp", "tensor"))
    cols, turned = P("dp", "tensor"), P("tensor", "dp")
    return jax.shard_map(
        on_device,
        mesh=mesh,
        in_specs=(tokens, cols, cols, cols, turned, cols, turned)
        + (vector,) * 9
        + (P("dp"), P("dp"), P("dp", None, None), P("dp", None, None), tokens),
        out_specs=(tokens, tokens, cols, cols, cols, turned, cols, turned) + (vector,) * 9,
        check_vma=False,
    )
```

profile of v0, /device:TPU:0, one launch (start us, length us, event | category | flops | bytes accessed | tf_op | source)
XLA Modules:
  0.0 324.8 jit_solution(8911351327430462203)
XLA Ops:
  7.2 0.0 copy-start
  7.2 0.0 all-gather.3.cloned.1.call-start
  7.3 1.7 pad_maximum_fusion
  9.0 0.0 all-gather.3.cloned.1.call-update
  9.0 0.0 reduce-scatter.2.cloned.1.call-start
  9.1 0.1 pad.4.clone
  9.2 0.0 copy-done
  9.2 0.1 dynamic_slice.30
  9.3 0.1 broadcast_in_dim.50
  9.4 0.1 reshape.227
  9.4 0.7 reshape.224
  10.2 0.5 broadcast.228
  10.7 0.7 fusion.15
  11.4 0.7 reshape.228
  12.2 0.2 slice_reduce_fusion.1
  12.4 0.2 convert_reduce_fusion.1
  12.6 0.1 copy.79
  12.7 0.1 copy.75
  12.8 0.8 dynamic_update_slice.7
  13.6 0.9 copy.83
  14.5 1.4 copy.85.key_info
  15.9 0.7 fusion.5
  16.6 0.1 select_reduce_fusion
  16.7 0.8 stack.43
  17.5 0.3 dynamic_update_slice.6
  17.8 0.8 broadcast_select_fusion.4
  18.6 0.8 broadcast_select_fusion
  19.4 0.9 concatenate.12
  20.3 0.6 pad_maximum_fusion.1.vec_ref
  20.9 63.3 %start.1 = (bf16[1,768,3072]{2,1,0:T(8,128)(2,1)}, bf16[1024,2304]{1,0:T(8,128)(2,1)}, bf16[1024,1536]{1,0:T(8,128)(2,1)}, f32[16,768]{1,0:T(8,128)}) custom-call(bf16[1,96,1536]{2,1,0:T(8,128)(2,1)} %bitcast.63, f32[16,768]{1,0:T(8,128)} %pad_maximum_fusion.1.vec_ref, bf16[1024,768]{1,0:T(8,128)(2,1)} %x_hbm.1), custom_call_target="tpu_custom_call" | custom-call | tf_op jit(solution)/shard_map/start/pallas_call | solution.py:381
  84.2 0.7 pad_add_fusion.bounds
  84.9 0.7 add_add_fusion.row_info
  85.6 41.2 %attend_forward.1 = (bf16[1024,768]{1,0:T(8,128)(2,1)}, f32[16,1024]{1,0:T(8,128)}) custom-call(s32[4,4]{1,0:T(4,128)} %pad_add_fusion.bounds, bf16[1024,2304]{1,0:T(8,128)(2,1)} %get-tuple-element.41.q_ref.qkv_ref, bf16[1024,2304]{1,0:T(8,128)(2,1)} %get-tuple-element.41.q_ref.qkv_ref, bf16[1024,1536]{1,0:T(8,128)(2,1)} %get-tuple-element.42.other_ref, ...), custom_call_target="tpu_custom_call" | custom-call | tf_op jit(solution)/shard_map/attend_forward/pallas_call | solution.py:550
  126.8 0.0 all-gather.3.cloned.1.call-done
  126.8 54.6 %middle.1 = (bf16[1024,768]{1,0:T(8,128)(2,1)}, f32[1024,768]{1,0:T(8,128)}, bf16[1024,768]{1,0:T(8,128)(2,1)}, bf16[1024,768]{1,0:T(8,128)(2,1)}, bf16[1024,307...) custom-call(bf16[1024,768]{1,0:T(8,128)(2,1)} %x_hbm.1, ...), custom_call_target="tpu_custom_call" | custom-call | tf_op jit(solution)/shard_map/middle/pallas_call | solution.py:846
  181.5 0.0 reduce-scatter.2.cloned.1.call-update
  181.5 53.1 %attend_backward.1 = (bf16[1024,768]{1,0:T(8,128)(2,1)}, bf16[2048,1536]{1,0:T(8,128)(2,1)}) custom-call(s32[4,4]{1,0:T(4,128)} %pad_add_fusion.bounds, bf16[1024,2304]{1,0:T(8,128)(2,1)} %get-tuple-element.41.q_ref.qkv_ref, bf16[1024,2304]{1,0:T(8,128)(2,1)} %get-tuple-element.41.q_ref.qkv_ref, bf16[1024,1536]{1,0:T(8,128)(2,1)} %get-tuple-element.42.other_ref, ...), custom_call_target="tpu_custom_call" | custom-call | tf_op jit(solution)/shard_map/attend_backward/pallas_call | solution.py:647
  234.6 71.6 %finish.1 = (f32[1024,768]{1,0:T(8,128)}, f32[96,192]{1,0:T(8,128)}, f32[96,192]{1,0:T(8,128)}, f32[96,192]{1,0:T(8,128)}, f32[96,192]{1,0:T(8,128)}, /*index=5*/f32[96,768]{1,0:T(8,128)}, f32[16,768]{1,0:T(8,128)}) custom-call(bf16[1024,768]{1,0:T(8,128)(2,1)} %x_hbm.1, bf16[1024,768]{1,0:T(8,128)(2,1)} %get-tuple-element.49.dq_hbm, ...), custom_call_target="tpu_custom_call" | custom-call | tf_op jit(solution)/shard_map/finish/pallas_call | solution.py:1172
  306.2 0.8 fusion.16
  307.0 0.6 dynamic_slice.34
  307.6 1.6 copy.87
  309.2 0.1 constant_dynamic-slice_fusion
  309.3 0.5 slice_bitcast_fusion
  309.8 0.0 reduce-scatter.2.cloned.1.call-done
  309.8 1.6 convert_bitcast_fusion
  311.5 0.0 copy-start.4
  311.5 0.0 copy-start.3
  311.5 0.0 copy-start.2
  311.5 0.0 copy-start.1
  311.5 3.8 %copy.98 = f32[1024,768]{1,0:T(8,128)} copy(f32[1024,768]{1,0:T(8,128)} %get-tuple-element.181) | data formatting | bytes 6291456
  315.3 0.0 copy-done.4
  315.3 0.6 copy.99
  315.9 0.0 copy-done.3
  315.9 0.6 copy.100
  316.6 0.0 copy-done.2
  316.6 0.6 copy.101
  317.2 0.0 copy-done.1
  317.2 0.7 copy.102
  (16 shorter events, 0.1 us)
Async XLA Ops:
  7.2 2.0 copy-start
  7.2 119.6 %all-gather.3.cloned.1.call-start = ((), (), s32[]{:S(2)}) async-start(), calls=%async_computation.2 | async-start | bytes 9732096 | tf_op jit(solution)/shard_map/all_gather | solution.py:1261
  9.0 300.8 %reduce-scatter.2.cloned.1.call-start = ((), (), s32[]{:S(2)}) async-start(), calls=%async_computation.1 | async-start | bytes 4866048 | tf_op jit(solution)/shard_map/reduce_scatter | solution.py:1283
  311.5 3.8 %copy-start.4 = (f32[96,192]{1,0:T(8,128)S(1)}, f32[96,192]{1,0:T(8,128)}, u32[]{:S(2)}) copy-start(f32[96,192]{1,0:T(8,128)} %get-tuple-element.182) | copy-start | bytes 221188
  311.5 4.5 %copy-start.3 = (f32[96,192]{1,0:T(8,128)S(1)}, f32[96,192]{1,0:T(8,128)}, u32[]{:S(2)}) copy-start(f32[96,192]{1,0:T(8,128)} %get-tuple-element.183) | copy-start | bytes 221188
  311.5 5.1 %copy-start.2 = (f32[96,192]{1,0:T(8,128)S(1)}, f32[96,192]{1,0:T(8,128)}, u32[]{:S(2)}) copy-start(f32[96,192]{1,0:T(8,128)} %get-tuple-element.184) | copy-start | bytes 221188
  311.5 5.8 %copy-start.1 = (f32[96,768]{1,0:T(8,128)S(1)}, f32[96,768]{1,0:T(8,128)}, u32[]{:S(2)}) copy-start(f32[96,768]{1,0:T(8,128)} %get-tuple-element.186) | copy-start | bytes 884740
Sparse Core Ops, SparseCore 0:
  11.5 94.5 all-gather.2
  181.6 112.4 reduce-scatter.1
where the time goes:
time: 325 us
  Pallas kernels  284 us (87%)
  local copies, waits for them, and re-layouts  19.2 us (6%)
  between operations  14.3 us (4%)
  other arithmetic  7.38 us (2%)
    pallas_call x1, Pallas kernels, finish(): pl.pallas_call(partial(finish_kernel, n), name='finish', in_specs=[anywhe...  71.6 us
    pallas_call x1, Pallas kernels, start(): pl.pallas_call(partial(start_kernel, n), name='start', in_specs=[inside]...  63.3 us
    pallas_call x1, Pallas kernels, middle(): pl.pallas_call(middle_kernel, name='middle', grid=(rows // ROWS,), in_spe...  54.6 us
    pallas_call x1, Pallas kernels, attend_backward(): pl.pallas_call(attend_backward_kernel, name='attend_backward', grid_spec=...  53.1 us
    pallas_call x1, Pallas kernels, attend_forward(): pl.pallas_call(attend_forward_kernel, name='attend_forward', grid_spec=pl...  41.2 us
    unnamed x18, local copies, waits for them, and re-layouts  9 us
  transfers between devices with their start and end apart: 2, of which 0 were waited for; matrix products, arithmetic and copies ran while one was open for 5% of the time, Pallas kernels for 71%

commit v1 on v0

--- a/solution.py
+++ b/solution.py
@@ -442,24 +442,50 @@
     return slice(lanes.start + third, lanes.stop + third)
 
 
-def fetch_keys(qkv_ref, other_ref, kv, sems):
+def key_tile(j, qkv_ref, other_ref, kv, sems):
     rows, third = other_ref.shape[0], other_ref.shape[1] // 4
-    half = lax.rem(lax.axis_index("tensor"), 2)
-    here = pl.ds(pl.multiple_of(half * rows, rows), rows)
-    there = pl.ds(pl.multiple_of((1 - half) * rows, rows), rows)
-    moves = [pltpu.make_async_copy(other_ref, kv.at[there, :], sems.at[2])]
-    for y in range(2):
-        moves.append(
-            pltpu.make_async_copy(
-                qkv_ref.at[:, (3 * y + 1) * third : (3 * y + 3) * third],
-                kv.at[here, 2 * y * third : 2 * (y + 1) * third],
-                sems.at[y],
-            )
+    here = pl.ds(pl.multiple_of(j * KT, KT), KT)
+    from_row = pl.ds(pl.multiple_of(lax.rem(j * KT, rows), KT), KT)
+    own = [
+        pltpu.make_async_copy(
+            qkv_ref.at[from_row, (3 * y + 1) * third : (3 * y + 3) * third],
+            kv.at[here, 2 * y * third : 2 * (y + 1) * third],
+            sems.at[y, j],
         )
-    for move in moves:
-        move.start()
-    for move in moves:
-        move.wait()
+        for y in range(2)
+    ]
+    far = pltpu.make_async_copy(other_ref.at[from_row, :], kv.at[here, :], sems.at[0, j])
+    is_own = (j * KT) // rows == lax.rem(lax.axis_index("tensor"), 2)
+    return is_own, own, far
+
+
+def fetch_keys(low, high, qkv_ref, other_ref, kv, sems, use):
+    @pl.loop(low, high)
+    def _(j):
+        is_own, own, far = key_tile(j, qkv_ref, other_ref, kv, sems)
+
+        @pl.when(is_own)
+        def _():
+            for move in own:
+                move.start()
+
+        @pl.when(jnp.logical_not(is_own))
+        def _():
+            far.start()
+
+    @pl.loop(low, high)
+    def _(j):
+        is_own, own, far = key_tile(j, qkv_ref, other_ref, kv, sems)
+
+        @pl.when(is_own)
+        def _():
+            for move in own:
+                move.wait()
+
+        @pl.when(jnp.logical_not(is_own))
+        def _():
+            far.wait()
+        use(j)
 
 
 def masked_pairs(source, target, lanes_of, pairs, scale):
@@ -493,7 +519,7 @@
 
 def attend_forward_kernel(
     bounds, q_ref, qkv_ref, other_ref, row_info, key_info, out_ref, log_ref,
-    q_pairs, kv_ref, v_turned, bias, top, total, acc, sems,
+    q_pairs, kv_ref, v_turned, bias, top, total, acc, scores, fades, lows, sems,
 ):
     step = pl.program_id(0)
     rows, width = out_ref.shape
@@ -502,11 +528,12 @@
 
     @pl.when(step == 0)
     def _():
-        fetch_keys(qkv_ref, other_ref, kv_ref, sems)
-        for j in range(tiles):
+        def turn(j):
             for p in range(pairs):
                 span = slice(p * PAIR, (p + 1) * PAIR)
-                v_turned[j, span, :] = kv_ref[j * KT : (j + 1) * KT, v_lanes(p, pairs)].T
+                v_turned[j, span, :] = kv_ref[pl.ds(pl.multiple_of(j * KT, KT), KT), v_lanes(p, pairs)].T
+
+        fetch_keys(bounds[0, 0], bounds[pl.num_programs(0) - 1, 1], qkv_ref, other_ref, kv_ref, sems, turn)
 
     masked_pairs(q_ref, q_pairs, partial(q_lanes, pairs=pairs), pairs, HD**-0.5)
     top[...] = jnp.full_like(top, NEGATIVE)
@@ -520,20 +547,23 @@
         keys_at = pl.multiple_of(j * KT, KT)
         for p in range(pairs):
             keys = kv_ref[pl.ds(keys_at, KT), k_lanes(p, pairs)]
-            scores = nt(keys, q_pairs[p])
-            for e in range(2):
-                h = 2 * p + e
-                mine = scores[:, e * rows : (e + 1) * rows] + bias[...]
-                before = top[h : h + 1, :]
-                now = jnp.maximum(before, jnp.max(mine, axis=0, keepdims=True))
-                fade = jnp.exp(before - now)
-                expos = jnp.exp(mine - now)
-                top[h : h + 1, :] = now
-                total[h : h + 1, :] = fade * total[h : h + 1, :] + jnp.sum(
-                    expos, axis=0, keepdims=True
-                )
-                span = slice(h * HD, (h + 1) * HD)
-                acc[span, :] = acc[span, :] * fade + nn(v_turned[j, span, :], expos.astype(BF))
+            scores[p] = nt(keys, q_pairs[p])
+        for h in range(2 * pairs):
+            p, e = divmod(h, 2)
+            mine = scores[p, :, e * rows : (e + 1) * rows] + bias[...]
+            before = top[h : h + 1, :]
+            now = jnp.maximum(before, jnp.max(mine, axis=0, keepdims=True))
+            fade = jnp.exp(before - now)
+            expos = jnp.exp(mine - now)
+            top[h : h + 1, :] = now
+            fades[h : h + 1, :] = fade
+            total[h : h + 1, :] = fade * total[h : h + 1, :] + jnp.sum(
+                expos, axis=0, keepdims=True
+            )
+            lows[h] = expos.astype(BF)
+        for h in range(2 * pairs):
+            span = slice(h * HD, (h + 1) * HD)
+            acc[span, :] = acc[span, :] * fades[h : h + 1, :] + nn(v_turned[j, span, :], lows[h])
 
     heads = width // HD
     for h in range(heads):
@@ -572,7 +602,10 @@
                 pltpu.VMEM((stat_rows, QT), F32),
                 pltpu.VMEM((stat_rows, QT), F32),
                 pltpu.VMEM((width, QT), F32),
-                pltpu.SemaphoreType.DMA((3,)),
+                pltpu.VMEM((width // PAIR, KT, 2 * QT), F32),
+                pltpu.VMEM((stat_rows, QT), F32),
+                pltpu.VMEM((width // HD, KT, QT), BF),
+                pltpu.SemaphoreType.DMA((2, keys // KT)),
             ],
         ),
         out_shape=[
@@ -585,7 +618,8 @@
 
 def attend_backward_kernel(
     bounds, q_ref, qkv_ref, other_ref, row_info, key_info, out_ref, log_ref, grad_ref,
-    dq_ref, dkv_ref, q_pairs, g_pairs, kv_ref, k_turned, bias, inner, dq_acc, dkv_acc, sems,
+    dq_ref, dkv_ref, q_pairs, g_pairs, kv_ref, k_turned, bias, inner, dq_acc, dkv_acc,
+    scores, changes, probs, grads, sems,
 ):
     step = pl.program_id(0)
     rows, width = out_ref.shape
@@ -594,20 +628,19 @@
 
     @pl.when(step == 0)
     def _():
-        fetch_keys(qkv_ref, other_ref, kv_ref, sems)
-        for j in range(tiles):
+        def turn(j):
             for p in range(pairs):
                 span = slice(p * PAIR, (p + 1) * PAIR)
-                k_turned[j, span, :] = kv_ref[j * KT : (j + 1) * KT, k_lanes(p, pairs)].T
+                k_turned[j, span, :] = kv_ref[pl.ds(pl.multiple_of(j * KT, KT), KT), k_lanes(p, pairs)].T
+
+        fetch_keys(bounds[0, 0], bounds[pl.num_programs(0) - 1, 1], qkv_ref, other_ref, kv_ref, sems, turn)
         dkv_acc[...] = jnp.zeros_like(dkv_acc)
 
     masked_pairs(q_ref, q_pairs, partial(q_lanes, pairs=pairs), pairs, HD**-0.5)
     masked_pairs(grad_ref, g_pairs, lambda p: slice(p * PAIR, (p + 1) * PAIR), pairs, None)
-    head_of = lax.broadcasted_iota(jnp.int32, (inner.shape[0], width), 1) // HD
-    row_of = lax.broadcasted_iota(jnp.int32, (inner.shape[0], width), 0)
-    chosen = jnp.where(head_of == row_of, 1.0, 0.0)
-    product = out_ref[...].astype(F32) * grad_ref[...].astype(F32)
-    inner[...] = nt(chosen, product, precision=lax.Precision.HIGHEST)
+    dq_acc[...] = (out_ref[...].astype(F32) * grad_ref[...].astype(F32)).T
+    for h in range(2 * pairs):
+        inner[h : h + 1, :] = jnp.sum(dq_acc[h * HD : (h + 1) * HD, :], axis=0, keepdims=True)
     dq_acc[...] = jnp.zeros_like(dq_acc)
     q_first = bounds[step, 2]
 
@@ -616,21 +649,21 @@
         tile_bias(j, q_first, row_info, key_info, bias)
         here = pl.ds(pl.multiple_of(j * KT, KT), KT)
         for p in range(pairs):
-            k_here, v_here = k_lanes(p, pairs), v_lanes(p, pairs)
-            scores = nt(kv_ref[here, k_here], q_pairs[p])
-            grad_probs = nt(kv_ref[here, v_here], g_pairs[p])
-            probs, grads = [], []
-            for e in range(2):
-                h = 2 * p + e
-                cols = slice(e * rows, (e + 1) * rows)
-                prob = jnp.exp(scores[:, cols] + bias[...] - log_ref[h : h + 1, :])
-                grad = (prob * (grad_probs[:, cols] - inner[h : h + 1, :])).astype(BF)
-                probs.append(prob.astype(BF))
-                grads.append(grad)
-                span = slice(h * HD, (h + 1) * HD)
-                dq_acc[span, :] += nn(k_turned[j, span, :], grad)
-            dkv_acc[here, k_here] += nn(jnp.concatenate(grads, axis=1), q_pairs[p])
-            dkv_acc[here, v_here] += nn(jnp.concatenate(probs, axis=1), g_pairs[p])
+            scores[p] = nt(kv_ref[here, k_lanes(p, pairs)], q_pairs[p])
+            changes[p] = nt(kv_ref[here, v_lanes(p, pairs)], g_pairs[p])
+        for h in range(2 * pairs):
+            p, e = divmod(h, 2)
+            cols = slice(e * rows, (e + 1) * rows)
+            prob = jnp.exp(scores[p, :, cols] + bias[...] - log_ref[h : h + 1, :])
+            probs[p, :, cols] = prob.astype(BF)
+            grads[p, :, cols] = (prob * (changes[p, :, cols] - inner[h : h + 1, :])).astype(BF)
+        for p in range(pairs):
+            dkv_acc[here, k_lanes(p, pairs)] += nn(grads[p], q_pairs[p])
+            dkv_acc[here, v_lanes(p, pairs)] += nn(probs[p], g_pairs[p])
+        for h in range(2 * pairs):
+            p, e = divmod(h, 2)
+            span = slice(h * HD, (h + 1) * HD)
+            dq_acc[span, :] += nn(k_turned[j, span, :], grads[p, :, e * rows : (e + 1) * rows])
 
     dq_ref[...] = (dq_acc[...] * HD**-0.5).T.astype(BF)
 
@@ -673,7 +706,11 @@
                 pltpu.VMEM((stat_rows, QT), F32),
                 pltpu.VMEM((width, QT), F32),
                 pltpu.VMEM((keys, 2 * width), F32),
-                pltpu.SemaphoreType.DMA((3,)),
+                pltpu.VMEM((width // PAIR, KT, 2 * QT), F32),
+                pltpu.VMEM((width // PAIR, KT, 2 * QT), F32),
+                pltpu.VMEM((width // PAIR, KT, 2 * QT), BF),
+                pltpu.VMEM((width // PAIR, KT, 2 * QT), BF),
+                pltpu.SemaphoreType.DMA((2, keys // KT)),
             ],
         ),
         out_shape=[

time: 325 us -> 306 us (0.942)
  Pallas kernels: 284 us -> 252 us
  waiting for transfers between devices: 0.06 us -> 11.6 us
    pallas_call x1, Pallas kernels: 53.1 us -> 34.3 us  [attend_backward(): pl.pallas_call(attend_backward_kernel, name='attend_backward', grid_spec=...]
    pallas_call x1, Pallas kernels: 41.2 us -> 23.3 us  [attend_forward(): pl.pallas_call(attend_forward_kernel, name='attend_forward', grid_spec=pl...]
    reduce_scatter x1, waiting for transfers between devices: 0.01 us -> 11.6 us  [on_device(): lax.psum_scatter(out_grad.reshape((dp * tp,) + out_grad.shape[2:]), ('dp'...]
    pallas_call x1, Pallas kernels: 71.6 us -> 76.3 us  [finish(): pl.pallas_call(partial(finish_kernel, n), name='finish', in_specs=[anywhe...]
  transfers between devices with their start and end apart: 2 -> 2, of which waited for: 0 -> 1; matrix products, arithmetic and copies ran while one was open for 5% -> 5% of each run, Pallas kernels for 71% -> 65%
where the time goes in v1:
time: 306 us; the launch traced here: 304 us
  Pallas kernels  252 us (82%)
  local copies, waits for them, and re-layouts  19.2 us (6%)
  between operations  14.3 us (5%)
  waiting for transfers between devices  11.6 us (4%)
  other arithmetic  7.37 us (2%)
    pallas_call x1, Pallas kernels, finish(): pl.pallas_call(partial(finish_kernel, n), name='finish', in_specs=[anywhe...  76.3 us
    pallas_call x1, Pallas kernels, start(): pl.pallas_call(partial(start_kernel, n), name='start', in_specs=[inside]...  63.3 us
    pallas_call x1, Pallas kernels, middle(): pl.pallas_call(middle_kernel, name='middle', grid=(rows // ROWS,), in_spe...  54.6 us
    pallas_call x1, Pallas kernels, attend_backward(): pl.pallas_call(attend_backward_kernel, name='attend_backward', grid_spec=...  34.3 us
    pallas_call x1, Pallas kernels, attend_forward(): pl.pallas_call(attend_forward_kernel, name='attend_forward', grid_spec=pl...  23.3 us
    reduce_scatter x1, waiting for transfers between devices, on_device(): lax.psum_scatter(out_grad.reshape((dp * tp,) + out_grad.shape[2:]), ('dp'...  11.6 us
    unnamed x18, local copies, waits for them, and re-layouts  9.01 us
  transfers between devices with their start and end apart: 2, of which 1 were waited for; matrix products, arithmetic and copies ran while one was open for 5% of the time, Pallas kernels for 65%

profile of v1, /device:TPU:0, one launch (start us, length us, event | category | flops | bytes accessed | tf_op | source)
XLA Modules:
  0.0 304.3 jit_solution(3269994379965000253)
XLA Ops:
  7.2 0.0 copy-start
  7.2 0.0 all-gather.3.cloned.1.call-start
  7.3 1.7 pad_maximum_fusion
  9.0 0.0 all-gather.3.cloned.1.call-update
  9.0 0.0 reduce-scatter.2.cloned.1.call-start
  9.1 0.1 pad.4.clone
  9.2 0.0 copy-done
  9.2 0.1 dynamic_slice.30
  9.3 0.1 broadcast_in_dim.50
  9.4 0.1 reshape.227
  9.4 0.7 reshape.224
  10.2 0.5 broadcast.228
  10.7 0.7 fusion.15
  11.4 0.7 reshape.228
  12.2 0.2 slice_reduce_fusion.1
  12.4 0.2 convert_reduce_fusion.1
  12.6 0.1 copy.79
  12.7 0.1 copy.75
  12.8 0.8 dynamic_update_slice.7
  13.6 0.9 copy.83
  14.5 1.4 copy.85.key_info
  15.9 0.7 fusion.5
  16.6 0.1 select_reduce_fusion
  16.7 0.8 stack.43
  17.5 0.3 dynamic_update_slice.6
  17.8 0.8 broadcast_select_fusion.4
  18.6 0.8 broadcast_select_fusion
  19.4 0.9 concatenate.12
  20.3 0.6 pad_maximum_fusion.1.vec_ref
  20.9 63.3 %start.1 = (bf16[1,768,3072]{2,1,0:T(8,128)(2,1)}, bf16[1024,2304]{1,0:T(8,128)(2,1)}, bf16[1024,1536]{1,0:T(8,128)(2,1)}, f32[16,768]{1,0:T(8,128)}) custom-call(bf16[1,96,1536]{2,1,0:T(8,128)(2,1)} %bitcast.63, f32[16,768]{1,0:T(8,128)} %pad_maximum_fusion.1.vec_ref, bf16[1024,768]{1,0:T(8,128)(2,1)} %x_hbm.1), custom_call_target="tpu_custom_call" | custom-call | tf_op jit(solution)/shard_map/start/pallas_call | solution.py:381
  84.2 0.7 pad_add_fusion.bounds
  84.9 0.7 add_add_fusion.row_info
  85.6 23.3 %attend_forward.1 = (bf16[1024,768]{1,0:T(8,128)(2,1)}, f32[16,1024]{1,0:T(8,128)}) custom-call(s32[4,4]{1,0:T(4,128)} %pad_add_fusion.bounds, bf16[1024,2304]{1,0:T(8,128)(2,1)} %get-tuple-element.41.q_ref.qkv_ref, bf16[1024,2304]{1,0:T(8,128)(2,1)} %get-tuple-element.41.q_ref.qkv_ref, bf16[1024,1536]{1,0:T(8,128)(2,1)} %get-tuple-element.42.other_ref, ...), custom_call_target="tpu_custom_call" | custom-call | tf_op jit(solution)/shard_map/attend_forward/pallas_call | solution.py:580
  108.9 0.0 all-gather.3.cloned.1.call-done
  108.9 54.6 %middle.1 = (bf16[1024,768]{1,0:T(8,128)(2,1)}, f32[1024,768]{1,0:T(8,128)}, bf16[1024,768]{1,0:T(8,128)(2,1)}, bf16[1024,768]{1,0:T(8,128)(2,1)}, bf16[1024,307...) custom-call(bf16[1024,768]{1,0:T(8,128)(2,1)} %x_hbm.1, ...), custom_call_target="tpu_custom_call" | custom-call | tf_op jit(solution)/shard_map/middle/pallas_call | solution.py:883
  163.5 0.0 reduce-scatter.2.cloned.1.call-update
  163.6 34.3 %attend_backward.1 = (bf16[1024,768]{1,0:T(8,128)(2,1)}, bf16[2048,1536]{1,0:T(8,128)(2,1)}) custom-call(s32[4,4]{1,0:T(4,128)} %pad_add_fusion.bounds, bf16[1024,2304]{1,0:T(8,128)(2,1)} %get-tuple-element.41.q_ref.qkv_ref, bf16[1024,2304]{1,0:T(8,128)(2,1)} %get-tuple-element.41.q_ref.qkv_ref, bf16[1024,1536]{1,0:T(8,128)(2,1)} %get-tuple-element.42.other_ref, ...), custom_call_target="tpu_custom_call" | custom-call | tf_op jit(solution)/shard_map/attend_backward/pallas_call | solution.py:680
  197.9 76.3 %finish.1 = (f32[1024,768]{1,0:T(8,128)}, f32[96,192]{1,0:T(8,128)}, f32[96,192]{1,0:T(8,128)}, f32[96,192]{1,0:T(8,128)}, f32[96,192]{1,0:T(8,128)}, /*index=5*/f32[96,768]{1,0:T(8,128)}, f32[16,768]{1,0:T(8,128)}) custom-call(bf16[1024,768]{1,0:T(8,128)(2,1)} %x_hbm.1, bf16[1024,768]{1,0:T(8,128)(2,1)} %get-tuple-element.49.dq_hbm, ...), custom_call_target="tpu_custom_call" | custom-call | tf_op jit(solution)/shard_map/finish/pallas_call | solution.py:1209
  274.2 0.8 fusion.16
  274.9 0.6 dynamic_slice.34
  275.5 1.6 copy.87
  277.2 0.1 constant_dynamic-slice_fusion
  277.2 0.5 slice_bitcast_fusion
  277.8 11.6 %reduce-scatter.2.cloned.1.call-done = bf16[1,96,768]{2,1,0:T(8,128)(2,1)} async-done(((bf16[32,96,768]{2,1,0:T(8,128)(2,1)}), bf16[1,96,768]{2,1,0:T(8,128)(2,1)}) %reduce-scatter.2.cloned.1.call-update) | async-done | bytes 147472 | tf_op jit(solution)/shard_map/reduce_scatter | solution.py:1320
  289.4 1.6 convert_bitcast_fusion
  291.0 0.0 copy-start.4
  291.0 0.0 copy-start.3
  291.0 0.0 copy-start.2
  291.0 0.0 copy-start.1
  291.0 3.8 %copy.98 = f32[1024,768]{1,0:T(8,128)} copy(f32[1024,768]{1,0:T(8,128)} %get-tuple-element.181) | data formatting | bytes 6291456
  294.8 0.0 copy-done.4
  294.8 0.6 copy.99
  295.5 0.0 copy-done.3
  295.5 0.6 copy.100
  296.1 0.0 copy-done.2
  296.1 0.6 copy.101
  296.8 0.0 copy-done.1
  296.8 0.7 copy.102
  (16 shorter events, 0.1 us)
Async XLA Ops:
  7.2 2.0 copy-start
  7.2 101.7 %all-gather.3.cloned.1.call-start = ((), (), s32[]{:S(2)}) async-start(), calls=%async_computation.2 | async-start | bytes 9732096 | tf_op jit(solution)/shard_map/all_gather | solution.py:1298
  9.0 280.4 %reduce-scatter.2.cloned.1.call-start = ((), (), s32[]{:S(2)}) async-start(), calls=%async_computation.1 | async-start | bytes 4866048 | tf_op jit(solution)/shard_map/reduce_scatter | solution.py:1320
  291.0 3.8 %copy-start.4 = (f32[96,192]{1,0:T(8,128)S(1)}, f32[96,192]{1,0:T(8,128)}, u32[]{:S(2)}) copy-start(f32[96,192]{1,0:T(8,128)} %get-tuple-element.182) | copy-start | bytes 221188
  291.0 4.5 %copy-start.3 = (f32[96,192]{1,0:T(8,128)S(1)}, f32[96,192]{1,0:T(8,128)}, u32[]{:S(2)}) copy-start(f32[96,192]{1,0:T(8,128)} %get-tuple-element.183) | copy-start | bytes 221188
  291.0 5.1 %copy-start.2 = (f32[96,192]{1,0:T(8,128)S(1)}, f32[96,192]{1,0:T(8,128)}, u32[]{:S(2)}) copy-start(f32[96,192]{1,0:T(8,128)} %get-tuple-element.184) | copy-start | bytes 221188
  291.0 5.8 %copy-start.1 = (f32[96,768]{1,0:T(8,128)S(1)}, f32[96,768]{1,0:T(8,128)}, u32[]{:S(2)}) copy-start(f32[96,768]{1,0:T(8,128)} %get-tuple-element.186) | copy-start | bytes 884740
Sparse Core Ops, SparseCore 0:
  11.5 94.4 all-gather.2
  163.7 125.6 reduce-scatter.1

commit v2 on v1

--- a/solution.py
+++ b/solution.py
@@ -12,6 +12,7 @@
 QT = 256
 KT = 128
 ROWS = 256
+BACK_ROWS = 256
 EPSILON = 1e-06
 NEGATIVE = -1e30
 MESH = pl.DeviceIdType.MESH
@@ -298,34 +299,28 @@
     save_w = pltpu.make_async_copy(out_ref, w_hbm, local_sem.at[1])
     save_w.start()
 
-    rows, width = x_ref.shape
+    width = x_ref.shape[1]
     third = width // 2
     vec_out[...] = vec_sent[len(partners)]
-    tiles = rows // ROWS
-
-    def keys_of(t, yi):
-        at = (pl.ds(pl.multiple_of(t * ROWS, ROWS), ROWS), slice((3 * yi + 1) * third, (3 * yi + 3) * third))
-        far = (at[0], slice(2 * yi * third, 2 * (yi + 1) * third))
-        return pltpu.make_async_remote_copy(qkv.at[at], other_hbm.at[far], ks.at[t, yi], kr.at[t, yi], device_id=w["sibling"], device_id_type=MESH)
-
-    @pl.loop(0, tiles)
-    def _(t):
-        at = pl.ds(pl.multiple_of(t * ROWS, ROWS), ROWS)
-        for yi in range(2):
-            both = nn(x_ref[at, :], out_ref[0, :, yi * wide + third : yi * wide + 3 * third])
-            first = (3 * yi + 1) * third
-            qkv[at, first : first + third] = both[:, :third].astype(BF)
-            bias = vec_out[1:2, yi * third : (yi + 1) * third]
-            qkv[at, first + third : first + 2 * third] = (both[:, third:] + bias).astype(BF)
-            keys_of(t, yi).start()
-
-    @pl.loop(0, tiles)
-    def _(t):
-        at = pl.ds(pl.multiple_of(t * ROWS, ROWS), ROWS)
-        for yi in range(2):
-            bias = vec_out[0:1, yi * third : (yi + 1) * third]
-            mine = nn(x_ref[at, :], out_ref[0, :, yi * wide : yi * wide + third]) + bias
-            qkv[at, 3 * yi * third : (3 * yi + 1) * third] = mine.astype(BF)
+
+    def keys_of(yi):
+        return pltpu.make_async_remote_copy(
+            qkv.at[:, (3 * yi + 1) * third : (3 * yi + 3) * third],
+            other_hbm.at[:, 2 * yi * third : 2 * (yi + 1) * third],
+            ks.at[yi], kr.at[yi], device_id=w["sibling"], device_id_type=MESH,
+        )
+
+    for yi in range(2):
+        first = (3 * yi + 1) * third
+        both = nn(x_ref[...], out_ref[0, :, yi * wide + third : yi * wide + 3 * third])
+        qkv[:, first : first + third] = both[:, :third].astype(BF)
+        bias = vec_out[1:2, yi * third : (yi + 1) * third]
+        qkv[:, first + third : first + 2 * third] = (both[:, third:] + bias).astype(BF)
+        keys_of(yi).start()
+    for yi in range(2):
+        first = 3 * yi * third
+        bias = vec_out[0:1, yi * third : (yi + 1) * third]
+        qkv[:, first : first + third] = (nn(x_ref[...], out_ref[0, :, yi * wide : yi * wide + third]) + bias).astype(BF)
 
     save_qkv = pltpu.make_async_copy(qkv, qkv_hbm, local_sem.at[2])
     save_qkv.start()
@@ -360,10 +355,8 @@
     for step in range(len(partners)):
         small_send(step).wait_send()
 
-    @pl.loop(0, tiles)
-    def _(t):
-        for yi in range(2):
-            keys_of(t, yi).wait()
+    for yi in range(2):
+        keys_of(yi).wait()
     save_w.wait()
     save_qkv.wait()
 
@@ -374,7 +367,6 @@
     parts, block, wide = mine.shape
     rows, width = layer_in.shape
     steps = 3 + (n - 1).bit_length()
-    tiles = rows // ROWS
     dma = pltpu.SemaphoreType.DMA
     anywhere, inside = pl.BlockSpec(memory_space=pl.ANY), pl.BlockSpec(memory_space=pltpu.VMEM)
     whole = (parts, dp * block, wide * tp // 2)
@@ -394,7 +386,7 @@
             pltpu.VMEM((rows, 3 * width), BF),
             pltpu.VMEM((steps + 1,) + vec.shape, F32), pltpu.VMEM((steps,) + vec.shape, F32),
             dma((3,)), dma((2,)), dma((1, 2, n)), dma((1, 2, n)), dma((1, n)), dma((1, n)),
-            dma((1, 2, n)), dma((1, 2, n)), dma((1, 4, n)), dma((1, 4, n)), dma((tiles, 2)), dma((tiles, 2)),
+            dma((1, 2, n)), dma((1, 2, n)), dma((1, 4, n)), dma((1, 4, n)), dma((2,)), dma((2,)),
             dma((steps,)), dma((steps,)),
         ],
         compiler_params=params_of(3),
@@ -799,105 +791,155 @@
     )
 
 
-def middle_kernel(
-    x_ref, attn_ref, cot_ref, w_ref, blocks_ref, vec_ref,
-    final_ref, first_grad, attn_grad, norm_low, unit_grad, proj_grad, out_grad,
-    sums, unit_sums, slope, hidden, outer,
+def fetch_blocks(blocks_hbm, blocks_ref, sems):
+    return [
+        pltpu.make_async_copy(blocks_hbm.at[:, t], blocks_ref.at[:, t], sems.at[t])
+        for t in range(blocks_ref.shape[1])
+    ]
+
+
+def begin_fetch(blocks_hbm, blocks_ref, sems):
+    @pl.when(pl.program_id(0) == 0)
+    def _():
+        for move in fetch_blocks(blocks_hbm, blocks_ref, sems):
+            move.start()
+
+
+def end_fetch(blocks_hbm, blocks_ref, sems):
+    @pl.when(pl.program_id(0) == 0)
+    def _():
+        for move in fetch_blocks(blocks_hbm, blocks_ref, sems):
+            move.wait()
+
+
+def unit_chunks(blocks_ref):
+    dp, tp, own_rows, both = blocks_ref.shape
+    units = both // 2
+    for t in range(tp):
+        w_in = lambda t=t: blocks_ref[:, t, :, :units].reshape(dp * own_rows, units)
+        w_out = lambda t=t: blocks_ref[:, t, :, units:].reshape(dp * own_rows, units)
+        yield t, slice(t * units, (t + 1) * units), w_in, w_out
+
+
+def forth_kernel(
+    x_ref, attn_ref, cot_ref, proj_0, proj_1, blocks_hbm, vec_ref,
+    final_ref, resid_out, grad_out, norm_low, slope, ffn_grad, out_grad, sums, hidden, outer, blocks_ref, sems,
 ):
-    width = x_ref.shape[1]
-    third = width // 2
-    wide = w_ref.shape[2] // 2
-    proj_cols = [slice((y + 1) * wide - third, (y + 1) * wide) for y in range(2)]
-    halves = [slice(y * third, (y + 1) * third) for y in range(2)]
-    own_units = blocks_ref.shape[3] // 2
-    chunks = [(t, slice(t * own_units, (t + 1) * own_units)) for t in range(blocks_ref.shape[1])]
-
-    def w_in(t):
-        return blocks_ref[:, t, :, :own_units].reshape(width, own_units)
-
-    def w_out(t):
-        return blocks_ref[:, t, :, own_units:].reshape(width, own_units)
-
+    begin_fetch(blocks_hbm, blocks_ref, sems)
     out_bias, last_bias, gain_1, shift_1, gain_2, shift_2 = (vec_ref[i : i + 1, :] for i in range(2, 8))
 
     @pl.when(pl.program_id(0) == 0)
     def _():
         sums[...] = jnp.zeros_like(sums)
-        unit_sums[...] = jnp.zeros_like(unit_sums)
         outer[...] = jnp.zeros_like(outer)
 
     resid = x_ref[...].astype(F32) + out_bias
-    for y in range(2):
-        resid += nt(attn_ref[:, halves[y]], w_ref[0, :, proj_cols[y]])
-    hat_1, inverse_1 = normalize(resid)
-    first_norm = hat_1 * gain_1 + shift_1
+    third = proj_0.shape[2]
+    resid += nt(attn_ref[:, :third], proj_0[0]) + nt(attn_ref[:, third:], proj_1[0])
+    resid_out[...] = resid
+    hat, _ = normalize(resid)
+    first_norm = hat * gain_1 + shift_1
     low = first_norm.astype(BF)
     norm_low[...] = low
     resid = first_norm + last_bias
-    for t, cols in chunks:
-        act, slope[:, cols] = gelu_and_slope(nn(low, w_in(t)) + vec_ref[8 + t : 9 + t, :own_units])
+    end_fetch(blocks_hbm, blocks_ref, sems)
+    for t, cols, w_in, w_out in unit_chunks(blocks_ref):
+        act, slope[:, cols] = gelu_and_slope(nn(low, w_in()) + vec_ref[8 + t : 9 + t, :])
         act = act.astype(BF)
         hidden[:, cols] = act
-        resid += nt(act, w_out(t))
-    hat_2, inverse_2 = normalize(resid)
-    final_ref[...] = (hat_2 * gain_2 + shift_2).astype(BF)
-
+        resid += nt(act, w_out())
+    hat, inverse = normalize(resid)
+    final_ref[...] = (hat * gain_2 + shift_2).astype(BF)
     cot = cot_ref[...].astype(F32)
-    grad = norm_backward(cot, hat_2, inverse_2, gain_2)
-    sums[6:7, :] += jnp.sum(cot * hat_2, axis=0, keepdims=True)
+    grad = norm_backward(cot, hat, inverse, gain_2)
+    sums[6:7, :] += jnp.sum(cot * hat, axis=0, keepdims=True)
     sums[7:8, :] += jnp.sum(cot, axis=0, keepdims=True)
     sums[3:4, :] += jnp.sum(grad, axis=0, keepdims=True)
+    grad_out[...] = grad
     low = grad.astype(BF)
+    ffn_grad[...] = low
     turned = low.T
-    for t, cols in chunks:
+    for t, cols, _, _ in unit_chunks(blocks_ref):
         outer[t] += nn(turned, hidden[:, cols])
-        act = (nn(low, w_out(t)) * slope[:, cols]).astype(BF)
+
+    @pl.when(pl.program_id(0) == pl.num_programs(0) - 1)
+    def _():
+        for t in range(out_grad.shape[1]):
+            out_grad[:, t] = outer[t].reshape(out_grad.shape[0], out_grad.shape[2], out_grad.shape[3]).astype(BF)
+
+
+def back_kernel(
+    resid_ref, grad_ref, ffn_grad, slope, proj_0, proj_1, blocks_hbm, vec_ref, sums_ref,
+    first_grad, attn_grad, unit_grad, proj_grad, sums, unit_sums, blocks_ref, sems,
+):
+    begin_fetch(blocks_hbm, blocks_ref, sems)
+    @pl.when(pl.program_id(0) == 0)
+    def _():
+        sums[...] = sums_ref[...]
+        unit_sums[...] = jnp.zeros_like(unit_sums)
+
+    hat, inverse = normalize(resid_ref[...])
+    low = ffn_grad[...]
+    grad = grad_ref[...]
+    end_fetch(blocks_hbm, blocks_ref, sems)
+    for t, cols, w_in, w_out in unit_chunks(blocks_ref):
+        act = (nn(low, w_out()) * slope[:, cols]).astype(BF)
         unit_grad[:, cols] = act
         unit_sums[0:1, cols] += jnp.sum(act.astype(F32), axis=0, keepdims=True)
-        grad += nt(act, w_in(t))
-    sums[4:5, :] += jnp.sum(grad * hat_1, axis=0, keepdims=True)
+        grad += nt(act, w_in())
+    sums[4:5, :] += jnp.sum(grad * hat, axis=0, keepdims=True)
     sums[5:6, :] += jnp.sum(grad, axis=0, keepdims=True)
-    grad = norm_backward(grad, hat_1, inverse_1, gain_1)
+    grad = norm_backward(grad, hat, inverse, vec_ref[4:5, :])
     sums[2:3, :] += jnp.sum(grad, axis=0, keepdims=True)
     first_grad[...] = grad
     low = grad.astype(BF)
     proj_grad[...] = low
-    for y in range(2):
-        attn_grad[:, halves[y]] = nn(low, w_ref[0, :, proj_cols[y]]).astype(BF)
-
-    @pl.when(pl.program_id(0) == pl.num_programs(0) - 1)
-    def _():
-        for t, _ in chunks:
-            out_grad[:, t] = outer[t].reshape(out_grad.shape[0], out_grad.shape[2], own_units).astype(BF)
+    third = proj_0.shape[2]
+    attn_grad[:, :third] = nn(low, proj_0[0]).astype(BF)
+    attn_grad[:, third:] = nn(low, proj_1[0]).astype(BF)
 
 
 def middle(layer_in, attn, output_grad, weights, blocks, vectors):
     rows, width = layer_in.shape
-    units = blocks.shape[1] * blocks.shape[3] // 2
-    tile = lambda w: pl.BlockSpec((ROWS, w), lambda i: (i, 0))
-    whole = lambda a: pl.BlockSpec(a.shape, lambda i: (0,) * len(a.shape), pipeline_mode=pl.Buffered(1))
+    tp, own_units = blocks.shape[1], blocks.shape[3] // 2
+    units = tp * own_units
+    once = dict(pipeline_mode=pl.Buffered(1))
+    whole = lambda a: pl.BlockSpec(a.shape, lambda i: (0,) * len(a.shape), **once)
     fixed = lambda w: pl.BlockSpec((8, w), lambda i: (0, 0))
     shape = lambda w, t: jax.ShapeDtypeStruct((rows, w), t)
-    out_grad = jax.ShapeDtypeStruct(blocks.shape[:3] + (blocks.shape[3] // 2,), BF)
-    out_spec = pl.BlockSpec(out_grad.shape, lambda i: (0, 0, 0, 0), pipeline_mode=pl.Buffered(1))
-    return pl.pallas_call(
-        middle_kernel,
-        name="middle",
+    sums_of = lambda w: jax.ShapeDtypeStruct((8, w), F32)
+    out_grad = jax.ShapeDtypeStruct(blocks.shape[:3] + (own_units,), BF)
+    third = width // 2
+    proj = [pl.BlockSpec((1, width, third), lambda i, y=y: (0, 0, 4 * y + 3), **once) for y in range(2)]
+    held = [pltpu.VMEM(blocks.shape, BF), pltpu.SemaphoreType.DMA((tp,))]
+    tile = lambda w: pl.BlockSpec((ROWS, w), lambda i: (i, 0))
+    layer_out, resid, grad_second, norm_low, slope, ffn_grad, out_grad, sums = pl.pallas_call(
+        forth_kernel,
+        name="middle_forth",
         grid=(rows // ROWS,),
-        in_specs=[tile(width)] * 3 + [whole(weights), whole(blocks), whole(vectors)],
-        out_specs=[tile(width)] * 4 + [tile(units), tile(width), out_spec, fixed(width), fixed(units)],
+        in_specs=[tile(width)] * 3 + proj + [pl.BlockSpec(memory_space=pl.ANY), whole(vectors)],
+        out_specs=[tile(width)] * 4 + [tile(units), tile(width), whole(out_grad), fixed(width)],
         out_shape=[
-            shape(width, BF), shape(width, F32), shape(width, BF), shape(width, BF), shape(units, BF), shape(width, BF),
-            out_grad,
-            jax.ShapeDtypeStruct((8, width), F32), jax.ShapeDtypeStruct((8, units), F32),
+            shape(width, BF), shape(width, F32), shape(width, F32), shape(width, BF), shape(units, F32),
+            shape(width, BF), out_grad, sums_of(width),
         ],
-        scratch_shapes=[
-            pltpu.VMEM((ROWS, units), F32),
-            pltpu.VMEM((ROWS, units), BF),
-            pltpu.VMEM((blocks.shape[1], width, units // blocks.shape[1]), F32),
+        scratch_shapes=[pltpu.VMEM((ROWS, units), BF), pltpu.VMEM((tp, width, own_units), F32)] + held,
+        compiler_params=params_of(),
+    )(layer_in, attn, output_grad, weights, weights, blocks, vectors)
+    tile = lambda w: pl.BlockSpec((BACK_ROWS, w), lambda i: (i, 0))
+    first_grad, attn_grad, unit_grad, proj_grad, sums, unit_sums = pl.pallas_call(
+        back_kernel,
+        name="middle_back",
+        grid=(rows // BACK_ROWS,),
+        in_specs=[tile(width)] * 3 + [tile(units)] + proj + [pl.BlockSpec(memory_space=pl.ANY), whole(vectors), whole(sums)],
+        out_specs=[tile(width)] * 2 + [tile(units), tile(width), fixed(width), fixed(units)],
+        out_shape=[
+            shape(width, F32), shape(width, BF), shape(units, BF), shape(width, BF), sums_of(width), sums_of(units),
         ],
+        scratch_shapes=held,
         compiler_params=params_of(),
-    )(layer_in, attn, output_grad, weights, blocks, vectors)
+    )(resid, grad_second, ffn_grad, slope, weights, weights, blocks, vectors, sums)
+    return layer_out, first_grad, attn_grad, norm_low, unit_grad, proj_grad, out_grad, sums, unit_sums
 
 
 def finish_kernel(

time: 306 us -> 293 us (0.958)
  waiting for transfers between devices: 11.6 us -> 0.06 us
    pallas_call x1, Pallas kernels: 76.3 us -> 62.9 us  [finish(): pl.pallas_call(partial(finish_kernel, n), name='finish', in_specs=[anywhe...]
    reduce_scatter x1, waiting for transfers between devices: 11.6 us -> 0.01 us  [on_device(): lax.psum_scatter(out_grad.reshape((dp * tp,) + out_grad.shape[2:]), ('dp'...]
    pallas_call x1 -> x2, Pallas kernels: 54.6 us -> 64.5 us  [the longest x1 40.7 us: middle(): pl.pallas_call(forth_kernel, name='middle_forth', grid=(rows // ROWS,), i...]
    unnamed x18 -> x20, local copies, waits for them, and re-layouts: 9.01 us -> 9.01 us
  transfers between devices with their start and end apart: 2 -> 2, of which waited for: 1 -> 0; matrix products, arithmetic and copies ran while one was open for 5% -> 6% of each run, Pallas kernels for 65% -> 72%
where the time goes in v2:
time: 293 us; the launch traced here: 291 us
  Pallas kernels  250 us (85%)
  local copies, waits for them, and re-layouts  19.2 us (7%)
  between operations  14.3 us (5%)
  other arithmetic  7.38 us (3%)
    pallas_call x1, Pallas kernels, finish(): pl.pallas_call(partial(finish_kernel, n), name='finish', in_specs=[anywhe...  62.9 us
    pallas_call x1, Pallas kernels, start(): pl.pallas_call(partial(start_kernel, n), name='start', in_specs=[inside]...  61.3 us
    pallas_call x1, Pallas kernels, middle(): pl.pallas_call(forth_kernel, name='middle_forth', grid=(rows // ROWS,), i...  40.7 us
    pallas_call x1, Pallas kernels, attend_backward(): pl.pallas_call(attend_backward_kernel, name='attend_backward', grid_spec=...  36.6 us
    pallas_call x1, Pallas kernels, attend_forward(): pl.pallas_call(attend_forward_kernel, name='attend_forward', grid_spec=pl...  25.1 us
    pallas_call x1, Pallas kernels, middle(): pl.pallas_call(back_kernel, name='middle_back', grid=(rows // BACK_ROWS,)...  23.8 us
    unnamed x20, local copies, waits for them, and re-layouts  9.01 us
  transfers between devices with their start and end apart: 2, of which 0 were waited for; matrix products, arithmetic and copies ran while one was open for 6% of the time, Pallas kernels for 72%

profile of v2, /device:TPU:0, one launch (start us, length us, event | category | flops | bytes accessed | tf_op | source)
XLA Modules:
  0.0 291.4 jit_solution(7920841851053777692)
XLA Ops:
  7.2 0.0 copy-start
  7.2 0.0 all-gather.3.cloned.1.call-start
  7.3 1.7 pad_maximum_fusion
  9.0 0.0 all-gather.3.cloned.1.call-update
  9.0 0.0 reduce-scatter.2.cloned.1.call-start
  9.1 0.1 pad.4.clone
  9.2 0.0 copy-done
  9.2 0.1 dynamic_slice.30
  9.3 0.1 broadcast_in_dim.50
  9.4 0.1 reshape.227
  9.4 0.7 reshape.224
  10.2 0.5 broadcast.228
  10.7 0.7 fusion.15
  11.4 0.7 reshape.228
  12.2 0.2 slice_reduce_fusion.1
  12.4 0.2 convert_reduce_fusion.1
  12.6 0.1 copy.79
  12.7 0.1 copy.75
  12.8 0.8 dynamic_update_slice.7
  13.7 0.9 copy.83
  14.5 1.4 copy.85.key_info
  15.9 0.7 fusion.5
  16.6 0.1 select_reduce_fusion
  16.7 0.8 stack.43
  17.5 0.3 dynamic_update_slice.6
  17.8 0.8 broadcast_select_fusion.4
  18.6 0.8 broadcast_select_fusion
  19.5 0.9 concatenate.12
  20.4 0.6 pad_maximum_fusion.1.vec_ref
  21.0 61.3 %start.1 = (bf16[1,768,3072]{2,1,0:T(8,128)(2,1)}, bf16[1024,2304]{1,0:T(8,128)(2,1)}, bf16[1024,1536]{1,0:T(8,128)(2,1)}, f32[16,768]{1,0:T(8,128)}) custom-call(bf16[1,96,1536]{2,1,0:T(8,128)(2,1)} %bitcast.64, f32[16,768]{1,0:T(8,128)} %pad_maximum_fusion.1.vec_ref, bf16[1024,768]{1,0:T(8,128)(2,1)} %x_hbm.1), custom_call_target="tpu_custom_call" | custom-call | tf_op jit(solution)/shard_map/start/pallas_call | solution.py:373
  82.3 0.7 pad_add_fusion.bounds
  83.0 0.7 add_add_fusion.row_info
  83.7 25.1 %attend_forward.1 = (bf16[1024,768]{1,0:T(8,128)(2,1)}, f32[16,1024]{1,0:T(8,128)}) custom-call(s32[4,4]{1,0:T(4,128)} %pad_add_fusion.bounds, bf16[1024,2304]{1,0:T(8,128)(2,1)} %get-tuple-element.46.q_ref.qkv_ref, bf16[1024,2304]{1,0:T(8,128)(2,1)} %get-tuple-element.46.q_ref.qkv_ref, bf16[1024,1536]{1,0:T(8,128)(2,1)} %get-tuple-element.47.other_ref, ...), custom_call_target="tpu_custom_call" | custom-call | tf_op jit(solution)/shard_map/attend_forward/pallas_call | solution.py:572
  108.8 0.0 all-gather.3.cloned.1.call-done
  108.8 40.7 %middle_forth.1 = (bf16[1024,768]{1,0:T(8,128)(2,1)}, f32[1024,768]{1,0:T(8,128)}, f32[1024,768]{1,0:T(8,128)}, bf16[1024,768]{1,0:T(8,128)(2,1)}, f32[1024,3072...) custom-call(bf16[1024,768]{1,0:T(8,128)(2,1)} %x_hbm.1, ...), custom_call_target="tpu_custom_call" | custom-call | tf_op jit(solution)/shard_map/middle_forth/pallas_call | solution.py:916
  149.5 0.0 reduce-scatter.2.cloned.1.call-update
  149.5 23.8 %middle_back.1 = (f32[1024,768]{1,0:T(8,128)}, bf16[1024,768]{1,0:T(8,128)(2,1)}, bf16[1024,3072]{1,0:T(8,128)(2,1)}, bf16[1024,768]{1,0:T(8,128)(2,1)}, f32[8,768]{1,0:T(8,128)}, /*index=5*/f32[8,3072]{1,0:T(8,128)}) custom-call(f32[1024,768]{1,0:T(8,128)} %get-tuple-element.53.resid_ref, f32[1024,768]{1,0:T(8,128)} %get-tuple-element.54.grad_ref, ...), custom_call_target="tpu_custom_call" | custom-call | tf_op jit(solution)/shard_map/middle_back/pallas_call | solution.py:930
  173.3 36.6 %attend_backward.1 = (bf16[1024,768]{1,0:T(8,128)(2,1)}, bf16[2048,1536]{1,0:T(8,128)(2,1)}) custom-call(s32[4,4]{1,0:T(4,128)} %pad_add_fusion.bounds, bf16[1024,2304]{1,0:T(8,128)(2,1)} %get-tuple-element.46.q_ref.qkv_ref, bf16[1024,2304]{1,0:T(8,128)(2,1)} %get-tuple-element.46.q_ref.qkv_ref, bf16[1024,1536]{1,0:T(8,128)(2,1)} %get-tuple-element.47.other_ref, ...), custom_call_target="tpu_custom_call" | custom-call | tf_op jit(solution)/shard_map/attend_backward/pallas_call | solution.py:672
  209.9 62.9 %finish.1 = (f32[1024,768]{1,0:T(8,128)}, f32[96,192]{1,0:T(8,128)}, f32[96,192]{1,0:T(8,128)}, f32[96,192]{1,0:T(8,128)}, f32[96,192]{1,0:T(8,128)}, /*index=5*/f32[96,768]{1,0:T(8,128)}, f32[16,768]{1,0:T(8,128)}) custom-call(bf16[1024,768]{1,0:T(8,128)(2,1)} %x_hbm.1, bf16[1024,768]{1,0:T(8,128)(2,1)} %get-tuple-element.59.dq_hbm, ...), custom_call_target="tpu_custom_call" | custom-call | tf_op jit(solution)/shard_map/finish/pallas_call | solution.py:1251
  272.8 0.8 fusion.16
  273.6 0.6 dynamic_slice.34
  274.2 1.6 copy.87
  275.8 0.1 constant_dynamic-slice_fusion
  275.9 0.5 slice_bitcast_fusion
  276.4 0.0 reduce-scatter.2.cloned.1.call-done
  276.4 1.6 convert_bitcast_fusion
  278.1 0.0 copy-start.1
  278.1 0.0 copy-start.5
  278.1 0.0 copy-start.4
  278.1 0.0 copy-start.3
  278.1 0.0 copy-start.2
  278.1 3.8 %copy.98 = f32[1024,768]{1,0:T(8,128)} copy(f32[1024,768]{1,0:T(8,128)} %get-tuple-element.191) | data formatting | bytes 6291456
  281.9 0.0 copy-done.5
  281.9 0.6 copy.99
  282.5 0.0 copy-done.4
  282.5 0.6 copy.100
  283.2 0.0 copy-done.3
  283.2 0.6 copy.101
  283.8 0.0 copy-done.2
  283.8 0.7 copy.102
  284.5 0.0 copy-done.1
  (16 shorter events, 0.1 us)
Async XLA Ops:
  7.2 2.0 copy-start
  7.2 101.6 %all-gather.3.cloned.1.call-start = ((), (), s32[]{:S(2)}) async-start(), calls=%async_computation.2 | async-start | bytes 9732096 | tf_op jit(solution)/shard_map/all_gather | solution.py:1340
  9.0 267.4 %reduce-scatter.2.cloned.1.call-start = ((), (), s32[]{:S(2)}) async-start(), calls=%async_computation.1 | async-start | bytes 4866048 | tf_op jit(solution)/shard_map/reduce_scatter | solution.py:1362
  278.1 6.5 %copy-start.1 = (s32[2,32,3]{1,0,2:T(2,128)S(1)}, s32[2,32,3]{1,0,2:T(2,128)}, u32[]{:S(2)}) copy-start(s32[2,32,3]{1,0,2:T(2,128)} %param.39) | copy-start | bytes 2308
  278.1 3.8 %copy-start.5 = (f32[96,192]{1,0:T(8,128)S(1)}, f32[96,192]{1,0:T(8,128)}, u32[]{:S(2)}) copy-start(f32[96,192]{1,0:T(8,128)} %get-tuple-element.192) | copy-start | bytes 221188
  278.1 4.5 %copy-start.4 = (f32[96,192]{1,0:T(8,128)S(1)}, f32[96,192]{1,0:T(8,128)}, u32[]{:S(2)}) copy-start(f32[96,192]{1,0:T(8,128)} %get-tuple-element.193) | copy-start | bytes 221188
  278.1 5.1 %copy-start.3 = (f32[96,192]{1,0:T(8,128)S(1)}, f32[96,192]{1,0:T(8,128)}, u32[]{:S(2)}) copy-start(f32[96,192]{1,0:T(8,128)} %get-tuple-element.194) | copy-start | bytes 221188
  278.1 5.8 %copy-start.2 = (f32[96,768]{1,0:T(8,128)S(1)}, f32[96,768]{1,0:T(8,128)}, u32[]{:S(2)}) copy-start(f32[96,768]{1,0:T(8,128)} %get-tuple-element.196) | copy-start | bytes 884740
Sparse Core Ops, SparseCore 0:
  11.5 94.1 all-gather.2
  149.6 110.2 reduce-scatter.1

commit v3 on v2

--- a/solution.py
+++ b/solution.py
@@ -135,8 +135,8 @@
 
 
 def start_kernel(
-    n, mine_ref, vec_ref, x_ref, w_hbm, qkv_hbm, other_hbm, vec_out,
-    out_ref, chip, sib, qkv, vec_sent, vec_got,
+    n, query_ref, key_ref, value_ref, proj_ref, vec_ref, x_ref, w_hbm, qkv_hbm, other_hbm, vec_out,
+    out_ref, chip, sib, mine_ref, qkv, vec_sent, vec_got,
     local_sem, pair_sem, zs, zr, as_, ar, bs, br, ss, sr, ks, kr, vs, vr,
 ):
     w = places()
@@ -145,6 +145,13 @@
     slab = block // 2
     up, down = {"dp": lax.rem(dp + 2, 2 * n), "tensor": rank}, {"dp": lax.rem(dp + 2 * n - 2, 2 * n), "tensor": rank}
     partners = [w["sibling"], w["second"], w["first"]] + line_jumps(dp, rank, z, n)
+    own_cols = query_ref.shape[1]
+    for i, ref in enumerate((query_ref, key_ref, value_ref, proj_ref)):
+        own_w = ref[...]
+        zero = jnp.zeros_like(own_w)
+        mine_ref[0, :, 2 * i * own_cols : 2 * (i + 1) * own_cols] = jnp.where(
+            core == 0, jnp.concatenate([own_w, zero], axis=1), jnp.concatenate([zero, own_w], axis=1)
+        )
     meet([up, down] + partners)
 
     pair = pltpu.make_async_remote_copy(mine_ref, sib, pair_sem.at[0], pair_sem.at[1], device_id=w["sibling"], device_id_type=MESH)
@@ -361,10 +368,12 @@
     save_qkv.wait()
 
 
-def start(mine, vec, layer_in):
+def start(own, vec, layer_in):
     dp, tp = lax.axis_size("dp"), lax.axis_size("tensor")
     n = dp // 2
-    parts, block, wide = mine.shape
+    block, own_cols = own[0].shape
+    parts, wide = 1, 2 * len(own) * own_cols
+    piece = pltpu.VMEM((parts, block, wide), BF)
     rows, width = layer_in.shape
     steps = 3 + (n - 1).bit_length()
     dma = pltpu.SemaphoreType.DMA
@@ -373,7 +382,7 @@
     return pl.pallas_call(
         partial(start_kernel, n),
         name="start",
-        in_specs=[inside] * 3,
+        in_specs=[inside] * 6,
         out_specs=[anywhere] * 3 + [inside],
         out_shape=[
             jax.ShapeDtypeStruct(whole, BF),
@@ -382,7 +391,7 @@
             jax.ShapeDtypeStruct(vec.shape, F32),
         ],
         scratch_shapes=[
-            pltpu.VMEM(whole, BF), pltpu.VMEM(mine.shape, BF), pltpu.VMEM(mine.shape, BF),
+            pltpu.VMEM(whole, BF), piece, piece, piece,
             pltpu.VMEM((rows, 3 * width), BF),
             pltpu.VMEM((steps + 1,) + vec.shape, F32), pltpu.VMEM((steps,) + vec.shape, F32),
             dma((3,)), dma((2,)), dma((1, 2, n)), dma((1, 2, n)), dma((1, n)), dma((1, n)),
@@ -390,15 +399,24 @@
             dma((steps,)), dma((steps,)),
         ],
         compiler_params=params_of(3),
-    )(mine, vec, layer_in)
+    )(*own, vec, layer_in)
 
 
 def in_tiles(block):
     return block % 32 == 0
 
 
-def start_plainly(mine, vec, layer_in):
+def start_plainly(own, vec, layer_in):
     dp, tp = lax.axis_size("dp"), lax.axis_size("tensor")
+    half = lax.rem(lax.axis_index("tensor"), 2)
+
+    def beside(one):
+        zero = jnp.zeros_like(one)
+        return jnp.concatenate(
+            [jnp.where(half == 0, one, zero), jnp.where(half == 0, zero, one)], axis=1
+        )
+
+    mine = jnp.concatenate([beside(one) for one in own], axis=1)[None]
     parts, block, wide = mine.shape
     width = layer_in.shape[1]
     third = width // 2
@@ -843,11 +861,31 @@
     norm_low[...] = low
     resid = first_norm + last_bias
     end_fetch(blocks_hbm, blocks_ref, sems)
-    for t, cols, w_in, w_out in unit_chunks(blocks_ref):
-        act, slope[:, cols] = gelu_and_slope(nn(low, w_in()) + vec_ref[8 + t : 9 + t, :])
-        act = act.astype(BF)
-        hidden[:, cols] = act
-        resid += nt(act, w_out())
+    chunks = list(unit_chunks(blocks_ref))
+    dp, tp, own_rows, both = blocks_ref.shape
+    units, sub = both // 2, 256
+    per = units // sub
+
+    def before(c):
+        first = c % per * sub
+        left = blocks_ref[:, c // per, :, first : first + sub].reshape(dp * own_rows, sub)
+        return nn(low, left) + vec_ref[8 + c // per : 9 + c // per, first : first + sub]
+
+    pre = before(0)
+    for c in range(tp * per):
+        after = before(c + 1) if c + 1 < tp * per else None
+        here = slice(c * sub, (c + 1) * sub)
+        act, slope[:, here] = gelu_and_slope(pre)
+        hidden[:, here] = act.astype(BF)
+        pre = after
+        done = c - 0
+        if done >= 0 and done % per == per - 1:
+            t, cols, _, w_out = chunks[done // per]
+            resid += nt(hidden[:, cols], w_out())
+    for c in range(tp * per - 0, tp * per):
+        if c % per == per - 1:
+            t, cols, _, w_out = chunks[c // per]
+            resid += nt(hidden[:, cols], w_out())
     hat, inverse = normalize(resid)
     final_ref[...] = (hat * gain_2 + shift_2).astype(BF)
     cot = cot_ref[...].astype(F32)
@@ -1330,18 +1368,10 @@
     third = width // 2
     half = lax.rem(lax.axis_index("tensor"), 2)
 
-    def beside(own):
-        zero = jnp.zeros_like(own)
-        return jnp.concatenate(
-            [jnp.where(half == 0, own, zero), jnp.where(half == 0, zero, own)], axis=1
-        )
-
     units_own = jnp.concatenate([inner_weight, outer_weight.T], axis=1)
     blocks = lax.all_gather(units_own, ("dp", "tensor"), axis=0, tiled=False)
     blocks = blocks.reshape(dp, tp, own_rows, 2 * own_units)
-    mine = jnp.concatenate(
-        [beside(w) for w in (query_weight, key_weight, value_weight, output_weight.T)], axis=1
-    )[None]
+    mine = (query_weight, key_weight, value_weight, output_weight.T)
     place = lax.axis_index("dp") * tp + lax.axis_index("tensor")
     one, own_bias = query_bias.shape[0], inner_bias.shape[0]
     small = jnp.stack([query_bias, value_bias, output_bias, outer_bias, first_gain, first_shift,

time: 293 us -> 294 us (level)
  Pallas kernels: 250 us -> 256 us
    pallas_call x1, Pallas kernels: 62.9 us -> 69.4 us  [finish(): pl.pallas_call(partial(finish_kernel, n), name='finish', in_specs=[anywhe...]
  transfers between devices with their start and end apart: 2 -> 2, of which waited for: 0 -> 0; matrix products, arithmetic and copies ran while one was open for 6% -> 5% of each run, Pallas kernels for 72% -> 73%
where the time goes in v3:
time: 294 us; the launch traced here: 295 us
  Pallas kernels  256 us (87%)
  local copies, waits for them, and re-layouts  19 us (6%)
  between operations  14.3 us (5%)
  other arithmetic  5.71 us (2%)
    pallas_call x1, Pallas kernels, finish(): pl.pallas_call(partial(finish_kernel, n), name='finish', in_specs=[anywhe...  69.4 us
    pallas_call x1, Pallas kernels, start(): pl.pallas_call(partial(start_kernel, n), name='start', in_specs=[inside]...  62.5 us
    pallas_call x1, Pallas kernels, middle(): pl.pallas_call(forth_kernel, name='middle_forth', grid=(rows // ROWS,), i...  40 us
    pallas_call x1, Pallas kernels, attend_backward(): pl.pallas_call(attend_backward_kernel, name='attend_backward', grid_spec=...  35.6 us
    pallas_call x1, Pallas kernels, attend_forward(): pl.pallas_call(attend_forward_kernel, name='attend_forward', grid_spec=pl...  24.4 us
    pallas_call x1, Pallas kernels, middle(): pl.pallas_call(back_kernel, name='middle_back', grid=(rows // BACK_ROWS,)...  23.8 us
    unnamed x20, local copies, waits for them, and re-layouts  9.63 us
  transfers between devices with their start and end apart: 2, of which 0 were waited for; matrix products, arithmetic and copies ran while one was open for 5% of the time, Pallas kernels for 73%

profile of v3, /device:TPU:0, one launch (start us, length us, event | category | flops | bytes accessed | tf_op | source)
XLA Modules:
  0.0 294.7 jit_solution(17517789669927966418)
XLA Ops:
  7.2 0.0 copy-start
  7.2 0.0 all-gather.3.cloned.1.call-start
  7.3 1.7 pad_maximum_fusion
  9.0 0.0 all-gather.3.cloned.1.call-update
  9.0 0.0 reduce-scatter.2.cloned.1.call-start
  9.1 0.1 pad.4.clone
  9.2 0.0 copy-done
  9.2 0.1 dynamic_slice.30
  9.3 0.1 broadcast_in_dim.46
  9.4 0.1 reshape.227
  9.4 0.7 reshape.224
  10.2 0.5 broadcast.207
  10.7 0.7 fusion.15
  11.4 0.7 reshape.228
  12.2 0.2 slice_reduce_fusion.1
  12.4 0.2 convert_reduce_fusion.1
  12.6 0.1 copy.76
  12.7 0.1 copy.72
  12.8 0.8 dynamic_update_slice.7
  13.6 1.5 copy.80
  15.2 1.4 copy.81.key_info
  16.6 0.7 fusion.5
  17.3 0.1 select_reduce_fusion
  17.4 0.8 stack.43
  18.2 0.3 dynamic_update_slice.6
  18.4 0.6 pad_maximum_fusion.1.vec_ref
  19.0 62.5 %start.1 = (bf16[1,768,3072]{2,1,0:T(8,128)(2,1)}, bf16[1024,2304]{1,0:T(8,128)(2,1)}, bf16[1024,1536]{1,0:T(8,128)(2,1)}, f32[16,768]{1,0:T(8,128)}) custom-call(bf16[96,192]{1,0:T(8,128)(2,1)} %query_ref.1, bf16[96,192]{1,0:T(8,128)(2,1)} %key_ref.1, bf16[96,192]{1,0:T(8,128)(2,1)} %value_ref.1, bf16[96,192]{1,0:T(8,128)(2,1)} %bitcast.60, ...), custom_call_target="tpu_custom_call" | custom-call | tf_op jit(solution)/shard_map/start/pallas_call | solution.py:382
  81.6 0.7 pad_add_fusion.bounds
  82.3 0.7 add_add_fusion.row_info
  83.0 24.4 %attend_forward.1 = (bf16[1024,768]{1,0:T(8,128)(2,1)}, f32[16,1024]{1,0:T(8,128)}) custom-call(s32[4,4]{1,0:T(4,128)} %pad_add_fusion.bounds, bf16[1024,2304]{1,0:T(8,128)(2,1)} %get-tuple-element.46.q_ref.qkv_ref, bf16[1024,2304]{1,0:T(8,128)(2,1)} %get-tuple-element.46.q_ref.qkv_ref, bf16[1024,1536]{1,0:T(8,128)(2,1)} %get-tuple-element.47.other_ref, ...), custom_call_target="tpu_custom_call" | custom-call | tf_op jit(solution)/shard_map/attend_forward/pallas_call | solution.py:590
  107.3 0.0 all-gather.3.cloned.1.call-done
  107.4 40.0 %middle_forth.1 = (bf16[1024,768]{1,0:T(8,128)(2,1)}, f32[1024,768]{1,0:T(8,128)}, f32[1024,768]{1,0:T(8,128)}, bf16[1024,768]{1,0:T(8,128)(2,1)}, f32[1024,3072...) custom-call(bf16[1024,768]{1,0:T(8,128)(2,1)} %x_hbm.1, ...), custom_call_target="tpu_custom_call" | custom-call | tf_op jit(solution)/shard_map/middle_forth/pallas_call | solution.py:954
  147.4 0.0 reduce-scatter.2.cloned.1.call-update
  147.4 23.8 %middle_back.1 = (f32[1024,768]{1,0:T(8,128)}, bf16[1024,768]{1,0:T(8,128)(2,1)}, bf16[1024,3072]{1,0:T(8,128)(2,1)}, bf16[1024,768]{1,0:T(8,128)(2,1)}, f32[8,768]{1,0:T(8,128)}, /*index=5*/f32[8,3072]{1,0:T(8,128)}) custom-call(f32[1024,768]{1,0:T(8,128)} %get-tuple-element.53.resid_ref, f32[1024,768]{1,0:T(8,128)} %get-tuple-element.54.grad_ref, ...), custom_call_target="tpu_custom_call" | custom-call | tf_op jit(solution)/shard_map/middle_back/pallas_call | solution.py:968
  171.1 35.6 %attend_backward.1 = (bf16[1024,768]{1,0:T(8,128)(2,1)}, bf16[2048,1536]{1,0:T(8,128)(2,1)}) custom-call(s32[4,4]{1,0:T(4,128)} %pad_add_fusion.bounds, bf16[1024,2304]{1,0:T(8,128)(2,1)} %get-tuple-element.46.q_ref.qkv_ref, bf16[1024,2304]{1,0:T(8,128)(2,1)} %get-tuple-element.46.q_ref.qkv_ref, bf16[1024,1536]{1,0:T(8,128)(2,1)} %get-tuple-element.47.other_ref, ...), custom_call_target="tpu_custom_call" | custom-call | tf_op jit(solution)/shard_map/attend_backward/pallas_call | solution.py:690
  206.7 69.4 %finish.1 = (f32[1024,768]{1,0:T(8,128)}, f32[96,192]{1,0:T(8,128)}, f32[96,192]{1,0:T(8,128)}, f32[96,192]{1,0:T(8,128)}, f32[96,192]{1,0:T(8,128)}, /*index=5*/f32[96,768]{1,0:T(8,128)}, f32[16,768]{1,0:T(8,128)}) custom-call(bf16[1024,768]{1,0:T(8,128)(2,1)} %x_hbm.1, bf16[1024,768]{1,0:T(8,128)(2,1)} %get-tuple-element.59.dq_hbm, ...), custom_call_target="tpu_custom_call" | custom-call | tf_op jit(solution)/shard_map/finish/pallas_call | solution.py:1289
  276.1 0.8 fusion.16
  276.9 0.6 dynamic_slice.34
  277.5 1.6 copy.83
  279.1 0.1 constant_dynamic-slice_fusion
  279.2 0.5 slice_bitcast_fusion
  279.7 0.0 reduce-scatter.2.cloned.1.call-done
  279.7 1.6 convert_bitcast_fusion
  281.4 0.0 copy-start.1
  281.4 0.0 copy-start.5
  281.4 0.0 copy-start.4
  281.4 0.0 copy-start.3
  281.4 0.0 copy-start.2
  281.4 3.8 %copy.94 = f32[1024,768]{1,0:T(8,128)} copy(f32[1024,768]{1,0:T(8,128)} %get-tuple-element.181) | data formatting | bytes 6291456
  285.2 0.0 copy-done.5
  285.2 0.6 copy.95
  285.9 0.0 copy-done.4
  285.9 0.6 copy.96
  286.5 0.0 copy-done.3
  286.5 0.6 copy.97
  287.2 0.0 copy-done.2
  287.2 0.7 copy.98
  287.9 0.0 copy-done.1
  (15 shorter events, 0.1 us)
Async XLA Ops:
  7.2 2.0 copy-start
  7.2 100.1 %all-gather.3.cloned.1.call-start = ((), (), s32[]{:S(2)}) async-start(), calls=%async_computation.2 | async-start | bytes 9732096 | tf_op jit(solution)/shard_map/all_gather | solution.py:1372
  9.0 270.7 %reduce-scatter.2.cloned.1.call-start = ((), (), s32[]{:S(2)}) async-start(), calls=%async_computation.1 | async-start | bytes 4866048 | tf_op jit(solution)/shard_map/reduce_scatter | solution.py:1392
  281.4 6.5 %copy-start.1 = (s32[2,32,3]{1,0,2:T(2,128)S(1)}, s32[2,32,3]{1,0,2:T(2,128)}, u32[]{:S(2)}) copy-start(s32[2,32,3]{1,0,2:T(2,128)} %param.39) | copy-start | bytes 2308
  281.4 3.8 %copy-start.5 = (f32[96,192]{1,0:T(8,128)S(1)}, f32[96,192]{1,0:T(8,128)}, u32[]{:S(2)}) copy-start(f32[96,192]{1,0:T(8,128)} %get-tuple-element.182) | copy-start | bytes 221188
  281.4 4.5 %copy-start.4 = (f32[96,192]{1,0:T(8,128)S(1)}, f32[96,192]{1,0:T(8,128)}, u32[]{:S(2)}) copy-start(f32[96,192]{1,0:T(8,128)} %get-tuple-element.183) | copy-start | bytes 221188
  281.4 5.1 %copy-start.3 = (f32[96,192]{1,0:T(8,128)S(1)}, f32[96,192]{1,0:T(8,128)}, u32[]{:S(2)}) copy-start(f32[96,192]{1,0:T(8,128)} %get-tuple-element.184) | copy-start | bytes 221188
  281.4 5.8 %copy-start.2 = (f32[96,768]{1,0:T(8,128)S(1)}, f32[96,768]{1,0:T(8,128)}, u32[]{:S(2)}) copy-start(f32[96,768]{1,0:T(8,128)} %get-tuple-element.186) | copy-start | bytes 884740
Sparse Core Ops, SparseCore 0:
  11.5 94.7 all-gather.2
  147.5 111.6 reduce-scatter.1

commit v4 on v3

--- a/solution.py
+++ b/solution.py
@@ -1155,6 +1155,10 @@
 
     @pl.loop(0, last_item + 4)
     def _(j):
+        @pl.when((j >= 1) & (j < last_item + 1))
+        def _():
+            stage_b(*item(j - 1))
+
         @pl.when(j < n)
         def _():
             k, zd = item(j)
@@ -1190,10 +1194,6 @@
             k, zd = item(j)
             compute_others(zd)
             to_sibling(0, zd).start()
-
-        @pl.when((j >= 1) & (j < last_item + 1))
-        def _():
-            stage_b(*item(j - 1))
 
         @pl.when((j >= 2) & (j < last_item + 2))
         def _():

time: 294 us -> 294 us (level)
  no operation moved by 1% of the time
where the time goes in v4:
time: 294 us
  Pallas kernels  255 us (87%)
  local copies, waits for them, and re-layouts  19 us (6%)
  between operations  14.3 us (5%)
  other arithmetic  5.71 us (2%)
    pallas_call x1, Pallas kernels, finish(): pl.pallas_call(partial(finish_kernel, n), name='finish', in_specs=[anywhe...  68.9 us
    pallas_call x1, Pallas kernels, start(): pl.pallas_call(partial(start_kernel, n), name='start', in_specs=[inside]...  62.5 us
    pallas_call x1, Pallas kernels, middle(): pl.pallas_call(forth_kernel, name='middle_forth', grid=(rows // ROWS,), i...  40 us
    pallas_call x1, Pallas kernels, attend_backward(): pl.pallas_call(attend_backward_kernel, name='attend_backward', grid_spec=...  35.3 us
    pallas_call x1, Pallas kernels, attend_forward(): pl.pallas_call(attend_forward_kernel, name='attend_forward', grid_spec=pl...  24.1 us
    pallas_call x1, Pallas kernels, middle(): pl.pallas_call(back_kernel, name='middle_back', grid=(rows // BACK_ROWS,)...  23.8 us
    unnamed x20, local copies, waits for them, and re-layouts  9.63 us
  transfers between devices with their start and end apart: 2, of which 0 were waited for; matrix products, arithmetic and copies ran while one was open for 5% of the time, Pallas kernels for 73%

profile of v4, /device:TPU:0, one launch (start us, length us, event | category | flops | bytes accessed | tf_op | source)
XLA Modules:
  0.0 293.7 jit_solution(4299554424779836694)
XLA Ops:
  7.2 0.0 copy-start
  7.2 0.0 all-gather.3.cloned.1.call-start
  7.3 1.7 pad_maximum_fusion
  9.0 0.0 all-gather.3.cloned.1.call-update
  9.0 0.0 reduce-scatter.2.cloned.1.call-start
  9.1 0.1 pad.4.clone
  9.2 0.0 copy-done
  9.2 0.1 dynamic_slice.30
  9.3 0.1 broadcast_in_dim.46
  9.4 0.1 reshape.227
  9.4 0.7 reshape.224
  10.2 0.5 broadcast.207
  10.7 0.7 fusion.15
  11.4 0.7 reshape.228
  12.2 0.2 slice_reduce_fusion.1
  12.4 0.2 convert_reduce_fusion.1
  12.6 0.1 copy.76
  12.7 0.1 copy.72
  12.8 0.8 dynamic_update_slice.7
  13.6 1.5 copy.80
  15.2 1.4 copy.81.key_info
  16.6 0.7 fusion.5
  17.3 0.1 select_reduce_fusion
  17.4 0.8 stack.43
  18.2 0.3 dynamic_update_slice.6
  18.4 0.6 pad_maximum_fusion.1.vec_ref
  19.0 62.5 %start.1 = (bf16[1,768,3072]{2,1,0:T(8,128)(2,1)}, bf16[1024,2304]{1,0:T(8,128)(2,1)}, bf16[1024,1536]{1,0:T(8,128)(2,1)}, f32[16,768]{1,0:T(8,128)}) custom-call(bf16[96,192]{1,0:T(8,128)(2,1)} %query_ref.1, bf16[96,192]{1,0:T(8,128)(2,1)} %key_ref.1, bf16[96,192]{1,0:T(8,128)(2,1)} %value_ref.1, bf16[96,192]{1,0:T(8,128)(2,1)} %bitcast.60, ...), custom_call_target="tpu_custom_call" | custom-call | tf_op jit(solution)/shard_map/start/pallas_call | solution.py:382
  81.6 0.7 pad_add_fusion.bounds
  82.3 0.7 add_add_fusion.row_info
  83.0 24.1 %attend_forward.1 = (bf16[1024,768]{1,0:T(8,128)(2,1)}, f32[16,1024]{1,0:T(8,128)}) custom-call(s32[4,4]{1,0:T(4,128)} %pad_add_fusion.bounds, bf16[1024,2304]{1,0:T(8,128)(2,1)} %get-tuple-element.46.q_ref.qkv_ref, bf16[1024,2304]{1,0:T(8,128)(2,1)} %get-tuple-element.46.q_ref.qkv_ref, bf16[1024,1536]{1,0:T(8,128)(2,1)} %get-tuple-element.47.other_ref, ...), custom_call_target="tpu_custom_call" | custom-call | tf_op jit(solution)/shard_map/attend_forward/pallas_call | solution.py:590
  107.1 0.0 all-gather.3.cloned.1.call-done
  107.1 40.0 %middle_forth.1 = (bf16[1024,768]{1,0:T(8,128)(2,1)}, f32[1024,768]{1,0:T(8,128)}, f32[1024,768]{1,0:T(8,128)}, bf16[1024,768]{1,0:T(8,128)(2,1)}, f32[1024,3072...) custom-call(bf16[1024,768]{1,0:T(8,128)(2,1)} %x_hbm.1, ...), custom_call_target="tpu_custom_call" | custom-call | tf_op jit(solution)/shard_map/middle_forth/pallas_call | solution.py:954
  147.1 0.0 reduce-scatter.2.cloned.1.call-update
  147.2 23.8 %middle_back.1 = (f32[1024,768]{1,0:T(8,128)}, bf16[1024,768]{1,0:T(8,128)(2,1)}, bf16[1024,3072]{1,0:T(8,128)(2,1)}, bf16[1024,768]{1,0:T(8,128)(2,1)}, f32[8,768]{1,0:T(8,128)}, /*index=5*/f32[8,3072]{1,0:T(8,128)}) custom-call(f32[1024,768]{1,0:T(8,128)} %get-tuple-element.53.resid_ref, f32[1024,768]{1,0:T(8,128)} %get-tuple-element.54.grad_ref, ...), custom_call_target="tpu_custom_call" | custom-call | tf_op jit(solution)/shard_map/middle_back/pallas_call | solution.py:968
  171.0 35.3 %attend_backward.1 = (bf16[1024,768]{1,0:T(8,128)(2,1)}, bf16[2048,1536]{1,0:T(8,128)(2,1)}) custom-call(s32[4,4]{1,0:T(4,128)} %pad_add_fusion.bounds, bf16[1024,2304]{1,0:T(8,128)(2,1)} %get-tuple-element.46.q_ref.qkv_ref, bf16[1024,2304]{1,0:T(8,128)(2,1)} %get-tuple-element.46.q_ref.qkv_ref, bf16[1024,1536]{1,0:T(8,128)(2,1)} %get-tuple-element.47.other_ref, ...), custom_call_target="tpu_custom_call" | custom-call | tf_op jit(solution)/shard_map/attend_backward/pallas_call | solution.py:690
  206.3 68.9 %finish.1 = (f32[1024,768]{1,0:T(8,128)}, f32[96,192]{1,0:T(8,128)}, f32[96,192]{1,0:T(8,128)}, f32[96,192]{1,0:T(8,128)}, f32[96,192]{1,0:T(8,128)}, /*index=5*/f32[96,768]{1,0:T(8,128)}, f32[16,768]{1,0:T(8,128)}) custom-call(bf16[1024,768]{1,0:T(8,128)(2,1)} %x_hbm.1, bf16[1024,768]{1,0:T(8,128)(2,1)} %get-tuple-element.59.dq_hbm, ...), custom_call_target="tpu_custom_call" | custom-call | tf_op jit(solution)/shard_map/finish/pallas_call | solution.py:1289
  275.2 0.8 fusion.16
  275.9 0.6 dynamic_slice.34
  276.5 1.6 copy.83
  278.1 0.1 constant_dynamic-slice_fusion
  278.2 0.5 slice_bitcast_fusion
  278.8 0.0 reduce-scatter.2.cloned.1.call-done
  278.8 1.6 convert_bitcast_fusion
  280.4 0.0 copy-start.1
  280.4 0.0 copy-start.5
  280.4 0.0 copy-start.4
  280.4 0.0 copy-start.3
  280.4 0.0 copy-start.2
  280.4 3.8 %copy.94 = f32[1024,768]{1,0:T(8,128)} copy(f32[1024,768]{1,0:T(8,128)} %get-tuple-element.181) | data formatting | bytes 6291456
  284.2 0.0 copy-done.5
  284.2 0.6 copy.95
  284.9 0.0 copy-done.4
  284.9 0.6 copy.96
  285.5 0.0 copy-done.3
  285.5 0.6 copy.97
  286.2 0.0 copy-done.2
  286.2 0.7 copy.98
  286.9 0.0 copy-done.1
  (15 shorter events, 0.1 us)
Async XLA Ops:
  7.2 2.0 copy-start
  7.2 99.9 %all-gather.3.cloned.1.call-start = ((), (), s32[]{:S(2)}) async-start(), calls=%async_computation.2 | async-start | bytes 9732096 | tf_op jit(solution)/shard_map/all_gather | solution.py:1372
  9.0 269.8 %reduce-scatter.2.cloned.1.call-start = ((), (), s32[]{:S(2)}) async-start(), calls=%async_computation.1 | async-start | bytes 4866048 | tf_op jit(solution)/shard_map/reduce_scatter | solution.py:1392
  280.4 6.5 %copy-start.1 = (s32[2,32,3]{1,0,2:T(2,128)S(1)}, s32[2,32,3]{1,0,2:T(2,128)}, u32[]{:S(2)}) copy-start(s32[2,32,3]{1,0,2:T(2,128)} %param.39) | copy-start | bytes 2308
  280.4 3.8 %copy-start.5 = (f32[96,192]{1,0:T(8,128)S(1)}, f32[96,192]{1,0:T(8,128)}, u32[]{:S(2)}) copy-start(f32[96,192]{1,0:T(8,128)} %get-tuple-element.182) | copy-start | bytes 221188
  280.4 4.5 %copy-start.4 = (f32[96,192]{1,0:T(8,128)S(1)}, f32[96,192]{1,0:T(8,128)}, u32[]{:S(2)}) copy-start(f32[96,192]{1,0:T(8,128)} %get-tuple-element.183) | copy-start | bytes 221188
  280.4 5.1 %copy-start.3 = (f32[96,192]{1,0:T(8,128)S(1)}, f32[96,192]{1,0:T(8,128)}, u32[]{:S(2)}) copy-start(f32[96,192]{1,0:T(8,128)} %get-tuple-element.184) | copy-start | bytes 221188
  280.4 5.8 %copy-start.2 = (f32[96,768]{1,0:T(8,128)S(1)}, f32[96,768]{1,0:T(8,128)}, u32[]{:S(2)}) copy-start(f32[96,768]{1,0:T(8,128)} %get-tuple-element.186) | copy-start | bytes 884740
Sparse Core Ops, SparseCore 0:
  11.5 94.7 all-gather.2
  147.3 110.9 reduce-scatter.1
